TPU v7x, 32 devices: a whole 2x2x4 slice. The times are simulated.
32 devices in a mesh: section: 2 (over x), dp: 4 (over y, core), tensor: 4 (over z).
Axes of the slice: x: 2, y: 2, z: 4, core: 2. Of those that a mesh axis runs over, the one named last changes fastest.
Arguments:
- block_input: bfloat16 [2, 4, 256, 1024], P(None, 'dp', 'tensor'), may hold values from -6 to 6
- seq_ids: int32 [2, 4, 256], P(None, 'dp'), may hold values from 0 to 7, never falling along the last dimension, each value on 1 to 192 neighbouring positions
- out_cotangent: bfloat16 [2, 4, 256, 1024], P(None, 'dp', 'tensor'), may hold values from -6 to 6
- qkv_weight: bfloat16 [2, 1024, 3, 1024], P('section', 'dp', None, 'tensor'), may hold values from -0.1875 to 0.1875
- qv_bias: bfloat16 [2, 2, 16, 64], P('section', None, 'tensor', 'dp'), may hold values from -3 to 3
- out_weight: bfloat16 [2, 1024, 1024], P('section', 'tensor', 'dp'), may hold values from -0.5 to 0.5
- out_bias: bfloat16 [2, 1024], P('section', 'dp'), may hold values from -3 to 3
- norm1_gain: bfloat16 [2, 1024], P('section', 'dp'), may hold values from 0.25 to 1.75
- norm1_bias: bfloat16 [2, 1024], P('section', 'dp'), may hold values from -3 to 3
- up_weight: bfloat16 [2, 1024, 4096], P('section', 'dp', 'tensor'), may hold values from -0.1875 to 0.1875
- up_bias: bfloat16 [2, 16, 256], P('section', 'tensor', 'dp'), may hold values from -3 to 3
- down_weight: bfloat16 [2, 4096, 1024], P('section', 'tensor', 'dp'), may hold values from -0.09375 to 0.09375
- down_bias: bfloat16 [2, 1024], P('section', 'dp'), may hold values from -3 to 3
- norm2_gain: bfloat16 [2, 1024], P('section', 'dp'), may hold values from 0.25 to 1.75
- norm2_bias: bfloat16 [2, 1024], P('section', 'dp'), may hold values from -3 to 3
Outputs:
- section_outputs: bfloat16 [2, 2, 4, 256, 1024], P('section', None, 'dp', 'tensor')
- input_grads: float32 [2, 2, 4, 256, 1024], P('section', None, 'dp', 'tensor')
- qkv_weight_grad: float32 [2, 1024, 3, 1024], P('section', 'dp', None, 'tensor')
- qv_bias_grad: float32 [2, 2, 16, 64], P('section', None, 'tensor', 'dp')
- out_weight_grad: float32 [2, 1024, 1024], P('section', 'tensor', 'dp')
- out_bias_grad: float32 [2, 1024], P('section', ('dp', 'tensor'))
- norm1_gain_grad: float32 [2, 1024], P('section', ('dp', 'tensor'))
- norm1_bias_grad: float32 [2, 1024], P('section', ('dp', 'tensor'))
- up_weight_grad: float32 [2, 1024, 4096], P('section', 'dp', 'tensor')
- up_bias_grad: float32 [2, 16, 256], P('section', 'tensor', 'dp')
- down_weight_grad: float32 [2, 4096, 1024], P('section', 'tensor', 'dp')
- down_bias_grad: float32 [2, 1024], P('section', ('dp', 'tensor'))
- norm2_gain_grad: float32 [2, 1024], P('section', ('dp', 'tensor'))
- norm2_bias_grad: float32 [2, 1024], P('section', ('dp', 'tensor'))
Inputs may be any that keep to these rules, and one draw needn't show every extreme that they name: `seq_ids`: along each pack of 256 tokens the ids never fall; every sequence has 1 to 192 tokens and one of each pack has exactly 192.
All inputs are finite; a program needn't handle non-finite values.
Results may differ from a plain program's by a relative error of at most 0.029.
Values may be sent and summed in bfloat16 or wider, within the bound.
A program may use at most 128 MiB of HBM per device.

v0:
```python
from functools import partial

import jax
import jax.numpy as jnp
from jax import lax
from jax.sharding import PartitionSpec as P


def shifted_2(value, axis, steps):
    count = lax.axis_size(axis)
    initial, last = (max(0, -steps), min(count, count - steps))
    return lax.ppermute(value, axis, [(source, source + steps) for source in range(initial, last)])


def gelu_exact(values):
    return 0.5 * values * (1.0 + jax.scipy.special.erf(values * 0.7071067811865476))


def gelu_slope(values):
    return (
        0.5 * (1.0 + jax.scipy.special.erf(values * 0.7071067811865476))
        + values * jnp.exp(-0.5 * values * values) * 0.3989422804014327
    )


def normalize(summed):
    center = summed - jnp.mean(summed, axis=-1, keepdims=True)
    scaled = lax.rsqrt(jnp.mean(center * center, axis=-1, keepdims=True) + 1e-12)
    return (center * scaled, scaled)


def norm_back(upstream, normed, scaled):
    return scaled * (
        upstream
        - jnp.mean(upstream, axis=-1, keepdims=True)
        - normed * jnp.mean(upstream * normed, axis=-1, keepdims=True)
    )


def masked_probs(queries, keys, same_seq):
    scores = jnp.einsum(
        "qhd,khd->hqk", queries, keys, preferred_element_type=jnp.float32
    ) * queries.shape[2] ** (-0.5)
    scores = jnp.where(same_seq[None], scores, -jnp.inf)
    largest = jnp.max(scores, axis=-1, keepdims=True)
    shifted = jnp.exp(scores - largest)
    return shifted / jnp.sum(shifted, axis=-1, keepdims=True)


def choose_section(last_section, from_last, from_first):
    return jnp.where(last_section, from_last, from_first)


def split_heads(qkv_held, which, head_count, head_size):
    return qkv_held[:, which].reshape(qkv_held.shape[0], head_count, head_size)


def layer_forward(local_rows, pack_ids, weights):
    qkv_mat, qv_shift, out_mat, up_mat, up_shift, down_mat, row_params = weights
    gathered = lax.all_gather(local_rows, "tensor", axis=0, tiled=True)
    tokens = gathered.shape[0]
    width = qkv_mat.shape[2]
    head_count = qv_shift.shape[1]
    head_size = qv_shift.shape[2]
    projected = jnp.einsum("tc,cjn->tjn", gathered, qkv_mat, preferred_element_type=jnp.float32)
    qv_wide = qv_shift.astype(jnp.float32).reshape(2, width)
    bias_rows = jnp.concatenate(
        [qv_wide[0:1], jnp.zeros((1, width), jnp.float32), qv_wide[1:2]], axis=0
    )
    qkv_held = (projected + bias_rows[None]).astype(jnp.bfloat16)
    queries = split_heads(qkv_held, 0, head_count, head_size)
    keys = split_heads(qkv_held, 1, head_count, head_size)
    values = split_heads(qkv_held, 2, head_count, head_size)
    same_seq = pack_ids[:, None] == pack_ids[None, :]
    attn_prob = masked_probs(queries, keys, same_seq)
    context = (
        jnp.einsum(
            "hqk,khd->qhd",
            attn_prob.astype(jnp.bfloat16),
            values,
            preferred_element_type=jnp.float32,
        )
        .reshape(tokens, width)
        .astype(jnp.bfloat16)
    )
    params_wide = row_params.astype(jnp.float32)
    attn_part = lax.psum_scatter(
        jnp.dot(context, out_mat, preferred_element_type=jnp.float32).astype(jnp.bfloat16),
        "tensor",
        scatter_dimension=0,
        tiled=True,
    ).astype(jnp.float32)
    resid_one = local_rows.astype(jnp.float32) + attn_part + params_wide[0]
    normed_one, scaled_one = normalize(resid_one)
    hidden_one = normed_one * params_wide[1] + params_wide[2]
    hidden_in = lax.all_gather(hidden_one.astype(jnp.bfloat16), "tensor", axis=0, tiled=True)
    pre_act = jnp.dot(hidden_in, up_mat, preferred_element_type=jnp.float32) + up_shift.astype(
        jnp.float32
    ).reshape(-1)
    activated = gelu_exact(pre_act).astype(jnp.bfloat16)
    resid_two = (
        hidden_one
        + lax.psum_scatter(
            jnp.dot(activated, down_mat, preferred_element_type=jnp.float32).astype(jnp.bfloat16),
            "tensor",
            scatter_dimension=0,
            tiled=True,
        ).astype(jnp.float32)
        + params_wide[3]
    )
    normed_two, scaled_two = normalize(resid_two)
    layer_out = (normed_two * params_wide[4] + params_wide[5]).astype(jnp.bfloat16)
    saved = (
        gathered,
        qkv_held,
        context,
        normed_one,
        scaled_one,
        hidden_in,
        pre_act,
        activated,
        normed_two,
        scaled_two,
    )
    return (layer_out, saved)


def layer_backward(upstream, pack_ids, weights, saved):
    qkv_mat, qv_shift, out_mat, up_mat, up_shift, down_mat, row_params = weights
    (
        gathered,
        qkv_held,
        context,
        normed_one,
        scaled_one,
        hidden_in,
        pre_act,
        activated,
        normed_two,
        scaled_two,
    ) = saved
    tokens = gathered.shape[0]
    width = qkv_mat.shape[2]
    head_count = qv_shift.shape[1]
    head_size = qv_shift.shape[2]
    params_wide = row_params.astype(jnp.float32)
    grad_two = norm_back(upstream * params_wide[4], normed_two, scaled_two)
    grad_full = lax.all_gather(grad_two.astype(jnp.bfloat16), "tensor", axis=0, tiled=True)
    down_grad = jnp.dot(activated.T, grad_full, preferred_element_type=jnp.float32)
    grad_pre = jnp.dot(grad_full, down_mat.T, preferred_element_type=jnp.float32) * gelu_slope(
        pre_act
    )
    grad_pre_held = grad_pre.astype(jnp.bfloat16)
    up_grad = jnp.dot(hidden_in.T, grad_pre_held, preferred_element_type=jnp.float32)
    grad_hidden = grad_two + lax.psum_scatter(
        jnp.dot(grad_pre_held, up_mat.T, preferred_element_type=jnp.float32).astype(jnp.bfloat16),
        "tensor",
        scatter_dimension=0,
        tiled=True,
    ).astype(jnp.float32)
    grad_one = norm_back(grad_hidden * params_wide[1], normed_one, scaled_one)
    resid_full = lax.all_gather(grad_one.astype(jnp.bfloat16), "tensor", axis=0, tiled=True)
    out_grad = jnp.dot(context.T, resid_full, preferred_element_type=jnp.float32)
    grad_context = (
        jnp.dot(resid_full, out_mat.T, preferred_element_type=jnp.float32)
        .astype(jnp.bfloat16)
        .reshape(tokens, head_count, head_size)
    )
    queries = split_heads(qkv_held, 0, head_count, head_size)
    keys = split_heads(qkv_held, 1, head_count, head_size)
    values = split_heads(qkv_held, 2, head_count, head_size)
    same_seq = pack_ids[:, None] == pack_ids[None, :]
    attn_prob = masked_probs(queries, keys, same_seq)
    grad_prob = jnp.einsum("qhd,khd->hqk", grad_context, values, preferred_element_type=jnp.float32)
    row_dots = jnp.sum(attn_prob * grad_prob, axis=-1, keepdims=True)
    grad_scores = (attn_prob * (grad_prob - row_dots) * head_size ** (-0.5)).astype(jnp.bfloat16)
    grad_queries = jnp.einsum("hqk,khd->qhd", grad_scores, keys, preferred_element_type=jnp.float32)
    grad_keys = jnp.einsum("hqk,qhd->khd", grad_scores, queries, preferred_element_type=jnp.float32)
    grad_values = jnp.einsum(
        "hqk,qhd->khd",
        attn_prob.astype(jnp.bfloat16),
        grad_context,
        preferred_element_type=jnp.float32,
    )
    qv_grad = jnp.stack([jnp.sum(grad_queries, axis=0), jnp.sum(grad_values, axis=0)])
    grad_qkv = (
        jnp.stack([grad_queries, grad_keys, grad_values], axis=1)
        .reshape(tokens, 3, width)
        .astype(jnp.bfloat16)
    )
    qkv_grad = jnp.einsum("tc,tjn->cjn", gathered, grad_qkv, preferred_element_type=jnp.float32)
    grad_inputs = grad_one + lax.psum_scatter(
        jnp.einsum("tjn,cjn->tc", grad_qkv, qkv_mat, preferred_element_type=jnp.float32).astype(
            jnp.bfloat16
        ),
        "tensor",
        scatter_dimension=0,
        tiled=True,
    ).astype(jnp.float32)
    row_grads = jnp.stack(
        [
            jnp.sum(grad_one, axis=0),
            jnp.sum(grad_hidden * normed_one, axis=0),
            jnp.sum(grad_hidden, axis=0),
            jnp.sum(grad_two, axis=0),
            jnp.sum(upstream * normed_two, axis=0),
            jnp.sum(upstream, axis=0),
        ]
    )
    up_shift_grad = jnp.sum(grad_pre, axis=0).reshape(up_shift.shape)
    return (
        grad_inputs,
        (qkv_grad, qv_grad, out_grad, up_grad, up_shift_grad, down_grad),
        row_grads,
    )


def shards(
    block_input,
    seq_ids,
    out_cotangent,
    qkv_weight,
    qv_bias,
    out_weight,
    out_bias,
    norm1_gain,
    norm1_bias,
    up_weight,
    up_bias,
    down_weight,
    down_bias,
    norm2_gain,
    norm2_bias,
):
    micro = block_input.shape[0]
    last_section = lax.axis_index("section") == 1
    pick_section = partial(choose_section, last_section)
    row_params = jnp.stack(
        [out_bias[0], norm1_gain[0], norm1_bias[0], down_bias[0], norm2_gain[0], norm2_bias[0]]
    )
    weights = (
        lax.all_gather(qkv_weight[0], "dp", axis=0, tiled=True),
        lax.all_gather(qv_bias[0], "dp", axis=2, tiled=True),
        lax.all_gather(out_weight[0], "dp", axis=1, tiled=True),
        lax.all_gather(up_weight[0], "dp", axis=0, tiled=True),
        lax.all_gather(up_bias[0], "dp", axis=1, tiled=True),
        lax.all_gather(down_weight[0], "dp", axis=1, tiled=True),
        lax.all_gather(row_params, "dp", axis=1, tiled=True),
    )
    received = jnp.zeros_like(block_input[0, 0])
    layer_outs = []
    layer_ins = []
    records = []
    tick_ids = []
    for forward_tick in range(micro + 1):
        section_rows = pick_section(received, block_input[min(forward_tick, micro - 1), 0])
        pack_ids = pick_section(
            seq_ids[max(forward_tick - 1, 0), 0], seq_ids[min(forward_tick, micro - 1), 0]
        )
        layer_out, saved = layer_forward(section_rows, pack_ids, weights)
        layer_outs.append(layer_out)
        layer_ins.append(section_rows)
        records.append(saved)
        tick_ids.append(pack_ids)
        if forward_tick < micro:
            received = shifted_2(layer_out, "section", 1)
    grad_back = jnp.zeros(block_input.shape[2:], jnp.float32)
    input_parts = []
    mat_totals = None
    row_totals = None
    for back_tick in range(micro + 1):
        later_tick = min(back_tick + 1, micro)
        earlier_tick = max(back_tick - 1, 0)
        pack_ids = pick_section(tick_ids[later_tick], tick_ids[earlier_tick])
        live_last = 1.0 if back_tick < micro else 0.0
        live_first = 1.0 if back_tick >= 1 else 0.0
        live_scale = jnp.where(last_section, live_last, live_first).astype(jnp.float32)
        upstream = (
            pick_section(out_cotangent[min(back_tick, micro - 1), 0].astype(jnp.float32), grad_back)
            * live_scale
        )
        saved = jax.tree.map(pick_section, records[later_tick], records[earlier_tick])
        grad_inputs, mat_grads, row_grads = layer_backward(upstream, pack_ids, weights, saved)
        input_parts.append(grad_inputs)
        if back_tick < micro:
            grad_back = shifted_2(grad_inputs.astype(jnp.bfloat16), "section", -1).astype(
                grad_inputs.dtype
            )
        if mat_totals is None:
            mat_totals = tuple(mat_grads)
            row_totals = row_grads
        else:
            mat_totals = tuple((running + fresh for running, fresh in zip(mat_totals, mat_grads)))
            row_totals = row_totals + row_grads
    mat_totals = (
        lax.psum_scatter(
            mat_totals[0].astype(jnp.bfloat16), "dp", scatter_dimension=0, tiled=True
        ).astype(jnp.float32),
        lax.psum_scatter(
            mat_totals[1].astype(jnp.bfloat16), "dp", scatter_dimension=2, tiled=True
        ).astype(jnp.float32),
        lax.psum_scatter(
            mat_totals[2].astype(jnp.bfloat16), "dp", scatter_dimension=1, tiled=True
        ).astype(jnp.float32),
        lax.psum_scatter(
            mat_totals[3].astype(jnp.bfloat16), "dp", scatter_dimension=0, tiled=True
        ).astype(jnp.float32),
        lax.psum_scatter(
            mat_totals[4].astype(jnp.bfloat16), "dp", scatter_dimension=1, tiled=True
        ).astype(jnp.float32),
        lax.psum_scatter(
            mat_totals[5].astype(jnp.bfloat16), "dp", scatter_dimension=1, tiled=True
        ).astype(jnp.float32),
    )
    row_totals = lax.psum_scatter(row_totals, ("dp", "tensor"), scatter_dimension=1, tiled=True)
    section_outputs = jnp.stack(
        [
            pick_section(layer_outs[micro_index + 1], layer_outs[micro_index])
            for micro_index in range(micro)
        ]
    )
    input_grads = jnp.stack(
        [
            pick_section(input_parts[micro_index], input_parts[micro_index + 1])
            for micro_index in range(micro)
        ]
    )
    return (
        section_outputs[None, :, None],
        input_grads[None, :, None],
        mat_totals[0][None],
        mat_totals[1][None],
        mat_totals[2][None],
        row_totals[0][None],
        row_totals[1][None],
        row_totals[2][None],
        mat_totals[3][None],
        mat_totals[4][None],
        mat_totals[5][None],
        row_totals[3][None],
        row_totals[4][None],
        row_totals[5][None],
    )


def solution(mesh):
    return jax.shard_map(
        shards,
        mesh=mesh,
        in_specs=(
            P(None, "dp", "tensor", None),
            P(None, "dp", None),
            P(None, "dp", "tensor", None),
            P("section", "dp", None, "tensor"),
            P("section", None, "tensor", "dp"),
            P("section", "tensor", "dp"),
            P("section", "dp"),
            P("section", "dp"),
            P("section", "dp"),
            P("section", "dp", "tensor"),
            P("section", "tensor", "dp"),
            P("section", "tensor", "dp"),
            P("section", "dp"),
            P("section", "dp"),
            P("section", "dp"),
        ),
        out_specs=(
            P("section", None, "dp", "tensor", None),
            P("section", None, "dp", "tensor", None),
            P("section", "dp", None, "tensor"),
            P("section", None, "tensor", "dp"),
            P("section", "tensor", "dp"),
            P("section", ("dp", "tensor")),
            P("section", ("dp", "tensor")),
            P("section", ("dp", "tensor")),
            P("section", "dp", "tensor"),
            P("section", "tensor", "dp"),
            P("section", "tensor", "dp"),
            P("section", ("dp", "tensor")),
            P("section", ("dp", "tensor")),
            P("section", ("dp", "tensor")),
        ),
        check_vma=False,
    )
```

profile of v0, /device:TPU:1, one launch (start us, length us, event | category | flops | bytes accessed | tf_op | source)
XLA Modules:
  0.0 853.6 jit_solution(12243912979129196675)
XLA Ops:
  10.0 6.1 all-gather.2
  17.5 15.3 %all-gather = bf16[1,1,256,1024]{3,2,1,0:T(8,128)(2,1)S(1)} all-gather(bf16[1,1,64,1024]{3,2,1,0:T(8,128)(2,1)S(1)} %slice_select_fusion), channel_id=2, replica_groups=mesh['section'=2,'dp'=4,'tensor'=4] {'tensor'}, dimensions={2}, use_global_device_ids=true | all-gather | bytes 655360 | tf_op jit(solution)/shard_map/all_gather | solution.py:60
  32.8 8.7 %all-gather.3 = bf16[1,256,1024]{2,1,0:T(8,128)(2,1)S(1)} all-gather(bf16[1,256,256]{2,1,0:T(8,128)(2,1)S(1)} %copy-done.66), channel_id=5, replica_groups=mesh['section'=2,'dp'=4,'tensor'=4] {'dp'}, dimensions={2}, use_global_device_ids=true | all-gather | bytes 655360 | tf_op jit(solution)/shard_map/all_gather | solution.py:244
  48.4 5.4 all-gather.5
  54.1 5.2 all_gather.61
  59.3 8.2 reduce-scatter.26.cloned.1.call-done
  70.7 12.5 %all_gather.62 = bf16[256,1024]{1,0:T(8,128)(2,1)S(1)} all-gather(bf16[64,1024]{1,0:T(8,128)(2,1)S(1)} %fusion.226), channel_id=1, replica_groups=mesh['section'=2,'dp'=4,'tensor'=4] {'tensor'}, dimensions={0}, use_global_device_ids=true | all-gather | bytes 655360 | tf_op jit(solution)/shard_map/all_gather | solution.py:96
  83.2 8.8 %all-gather.13.cloned.1.call-done = bf16[1,1024,1024]{2,1,0:T(8,128)(2,1)} async-done(((bf16[1,256,1024]{2,1,0:T(8,128)(2,1)}), bf16[1,1024,1024]{2,1,0:T(8,128)(2,1)}) %all-gather.13.cloned.1.call-update) | async-done | bytes 2097168 | tf_op jit(solution)/shard_map/all_gather | solution.py:245
  92.0 3.3 fusion.81
  95.2 21.0 %all-gather.15.cloned.1.call-done = bf16[1,1024,1024]{2,1,0:T(8,128)(2,1)} async-done(((bf16[1,1024,256]{2,1,0:T(8,128)(2,1)}), bf16[1,1024,1024]{2,1,0:T(8,128)(2,1)}) %all-gather.15.cloned.1.call-update) | async-done | bytes 2097168 | tf_op jit(solution)/shard_map/all_gather | solution.py:247
  116.2 3.4 fusion.117
  120.3 19.3 %reduce-scatter.28.cloned.1.call-done = bf16[64,1024]{1,0:T(8,128)(2,1)} async-done(((bf16[256,1024]{1,0:T(8,128)(2,1)}), bf16[64,1024]{1,0:T(8,128)(2,1)}) %reduce-scatter.28.cloned.1.call-update) | async-done | bytes 131088 | tf_op jit(solution)/shard_map/reduce_scatter | solution.py:103
  141.3 3.1 collective-permute-start
  146.4 13.2 %all_gather.66 = bf16[256,1024]{1,0:T(8,128)(2,1)S(1)} all-gather(bf16[64,1024]{1,0:T(8,128)(2,1)S(1)} %bitcast_select_fusion.5), channel_id=1, replica_groups=mesh['section'=2,'dp'=4,'tensor'=4] {'tensor'}, dimensions={0}, use_global_device_ids=true | all-gather | bytes 655360 | tf_op jit(solution)/shard_map/all_gather | solution.py:60
  166.1 24.2 %reduce-scatter.30.cloned.1.call-done = bf16[64,1024]{1,0:T(8,128)(2,1)} async-done(((bf16[256,1024]{1,0:T(8,128)(2,1)}), bf16[64,1024]{1,0:T(8,128)(2,1)}) %reduce-scatter.30.cloned.1.call-update) | async-done | bytes 131088 | tf_op jit(solution)/shard_map/reduce_scatter | solution.py:87
  193.5 12.4 %all_gather.67 = bf16[256,1024]{1,0:T(8,128)(2,1)S(1)} all-gather(bf16[64,1024]{1,0:T(8,128)(2,1)S(1)} %fusion.227), channel_id=1, replica_groups=mesh['section'=2,'dp'=4,'tensor'=4] {'tensor'}, dimensions={0}, use_global_device_ids=true | all-gather | bytes 655360 | tf_op jit(solution)/shard_map/all_gather | solution.py:96
  205.9 3.5 fusion.84
  209.4 2.8 fusion.120
  213.0 22.6 %reduce-scatter.32.cloned.1.call-done = bf16[64,1024]{1,0:T(8,128)(2,1)} async-done(((bf16[256,1024]{1,0:T(8,128)(2,1)}), bf16[64,1024]{1,0:T(8,128)(2,1)}) %reduce-scatter.32.cloned.1.call-update) | async-done | bytes 131088 | tf_op jit(solution)/shard_map/reduce_scatter | solution.py:103
  239.8 3.1 collective-permute-start.1
  245.7 12.9 %all_gather.68 = bf16[256,1024]{1,0:T(8,128)(2,1)S(1)} all-gather(bf16[64,1024]{1,0:T(8,128)(2,1)S(1)} %bitcast_select_fusion.4), channel_id=1, replica_groups=mesh['section'=2,'dp'=4,'tensor'=4] {'tensor'}, dimensions={0}, use_global_device_ids=true | all-gather | bytes 655360 | tf_op jit(solution)/shard_map/all_gather | solution.py:60
  258.6 2.9 broadcast_select_fusion
  266.7 2.6 convolution_convert_fusion.9
  273.2 14.7 %all_gather.70 = bf16[256,1024]{1,0:T(8,128)(2,1)S(1)} all-gather(bf16[64,1024]{1,0:T(8,128)(2,1)S(1)} %get-tuple-element.111), channel_id=1, replica_groups=mesh['section'=2,'dp'=4,'tensor'=4] {'tensor'}, dimensions={0}, use_global_device_ids=true | all-gather | bytes 655360 | tf_op jit(solution)/shard_map/all_gather | solution.py:148
  287.9 3.7 fusion.332
  294.1 3.4 reduce-scatter.34.cloned.1.call-done
  300.4 22.5 %reduce-scatter.38.cloned.1.call-done = bf16[64,1024]{1,0:T(8,128)(2,1)} async-done(((bf16[256,1024]{1,0:T(8,128)(2,1)}), bf16[64,1024]{1,0:T(8,128)(2,1)}) %reduce-scatter.38.cloned.1.call-update) | async-done | bytes 131088 | tf_op jit(solution)/shard_map/reduce_scatter | solution.py:155
  322.9 2.9 multiply_reduce_fusion.7
  325.8 12.4 %all_gather.69 = bf16[256,1024]{1,0:T(8,128)(2,1)S(1)} all-gather(bf16[64,1024]{1,0:T(8,128)(2,1)S(1)} %get-tuple-element.171), channel_id=1, replica_groups=mesh['section'=2,'dp'=4,'tensor'=4] {'tensor'}, dimensions={0}, use_global_device_ids=true | all-gather | bytes 655360 | tf_op jit(solution)/shard_map/all_gather | solution.py:96
  344.6 2.9 fusion.322
  349.7 16.7 %reduce-scatter.36.cloned.1.call-done = bf16[64,1024]{1,0:T(8,128)(2,1)} async-done(((bf16[256,1024]{1,0:T(8,128)(2,1)}), bf16[64,1024]{1,0:T(8,128)(2,1)}) %reduce-scatter.36.cloned.1.call-update) | async-done | bytes 131088 | tf_op jit(solution)/shard_map/reduce_scatter | solution.py:103
  368.4 12.4 %all_gather.71 = bf16[256,1024]{1,0:T(8,128)(2,1)S(1)} all-gather(bf16[64,1024]{1,0:T(8,128)(2,1)S(1)} %convert_element_type.322), channel_id=1, replica_groups=mesh['section'=2,'dp'=4,'tensor'=4] {'tensor'}, dimensions={0}, use_global_device_ids=true | all-gather | bytes 655360 | tf_op jit(solution)/shard_map/all_gather | solution.py:162
  382.6 3.0 fusion.314
  388.0 3.4 convolution_convert_fusion.7
  391.5 4.0 fusion.313
  400.4 3.0 fusion.105
  405.3 21.5 %reduce-scatter.40.cloned.1.call-done = bf16[64,1024]{1,0:T(8,128)(2,1)} async-done(((bf16[256,1024]{1,0:T(8,128)(2,1)}), bf16[64,1024]{1,0:T(8,128)(2,1)}) %reduce-scatter.40.cloned.1.call-update) | async-done | bytes 131088 | tf_op jit(solution)/shard_map/reduce_scatter | solution.py:192
  430.5 3.2 collective-permute-done.2
  437.1 13.6 %all_gather.72 = bf16[256,1024]{1,0:T(8,128)(2,1)S(1)} all-gather(bf16[64,1024]{1,0:T(8,128)(2,1)S(1)} %get-tuple-element.107), channel_id=1, replica_groups=mesh['section'=2,'dp'=4,'tensor'=4] {'tensor'}, dimensions={0}, use_global_device_ids=true | all-gather | bytes 655360 | tf_op jit(solution)/shard_map/all_gather | solution.py:148
  450.8 3.5 fusion.333
  460.4 3.0 fusion.325
  463.5 15.4 %reduce-scatter.42.cloned.1.call-done = bf16[64,1024]{1,0:T(8,128)(2,1)} async-done(((bf16[256,1024]{1,0:T(8,128)(2,1)}), bf16[64,1024]{1,0:T(8,128)(2,1)}) %reduce-scatter.42.cloned.1.call-update) | async-done | bytes 131088 | tf_op jit(solution)/shard_map/reduce_scatter | solution.py:155
  482.5 12.4 %all_gather.73 = bf16[256,1024]{1,0:T(8,128)(2,1)S(1)} all-gather(bf16[64,1024]{1,0:T(8,128)(2,1)S(1)} %convert_element_type.336), channel_id=1, replica_groups=mesh['section'=2,'dp'=4,'tensor'=4] {'tensor'}, dimensions={0}, use_global_device_ids=true | all-gather | bytes 655360 | tf_op jit(solution)/shard_map/all_gather | solution.py:162
  496.8 3.0 fusion.312
  502.1 3.4 convolution_convert_fusion.5
  505.5 3.9 fusion.311
  512.9 2.9 fusion.102
  515.9 23.4 %reduce-scatter.44.cloned.1.call-done = bf16[64,1024]{1,0:T(8,128)(2,1)} async-done(((bf16[256,1024]{1,0:T(8,128)(2,1)}), bf16[64,1024]{1,0:T(8,128)(2,1)}) %reduce-scatter.44.cloned.1.call-update) | async-done | bytes 131088 | tf_op jit(solution)/shard_map/reduce_scatter | solution.py:192
  542.5 4.6 collective-permute-done.3
  549.9 13.5 %all_gather.74 = bf16[256,1024]{1,0:T(8,128)(2,1)S(1)} all-gather(bf16[64,1024]{1,0:T(8,128)(2,1)S(1)} %get-tuple-element.103), channel_id=1, replica_groups=mesh['section'=2,'dp'=4,'tensor'=4] {'tensor'}, dimensions={0}, use_global_device_ids=true | all-gather | bytes 655360 | tf_op jit(solution)/shard_map/all_gather | solution.py:148
  563.4 3.8 fusion.331
  571.2 3.0 fusion.328
  576.4 15.4 %reduce-scatter.46.cloned.1.call-done = bf16[64,1024]{1,0:T(8,128)(2,1)} async-done(((bf16[256,1024]{1,0:T(8,128)(2,1)}), bf16[64,1024]{1,0:T(8,128)(2,1)}) %reduce-scatter.46.cloned.1.call-update) | async-done | bytes 131088 | tf_op jit(solution)/shard_map/reduce_scatter | solution.py:155
  595.3 12.4 %all_gather.75 = bf16[256,1024]{1,0:T(8,128)(2,1)S(1)} all-gather(bf16[64,1024]{1,0:T(8,128)(2,1)S(1)} %convert_element_type.348), channel_id=1, replica_groups=mesh['section'=2,'dp'=4,'tensor'=4] {'tensor'}, dimensions={0}, use_global_device_ids=true | all-gather | bytes 655360 | tf_op jit(solution)/shard_map/all_gather | solution.py:162
  611.3 2.6 convolution_convert_fusion.3
  614.1 2.7 fusion.309
  621.3 3.1 fusion.99
  641.1 3.7 add_convert_fusion
  649.4 48.5 %reduce-scatter.60.cloned.1.call-done = f32[64,6]{1,0:T(8,128)} async-done(((f32[1024,6]{1,0:T(8,128)}), f32[64,6]{1,0:T(8,128)}) %reduce-scatter.60.cloned.1.call-update) | async-done | bytes 1552
  702.6 19.4 %reduce-scatter.48.cloned.1.call-done = bf16[64,1024]{1,0:T(8,128)(2,1)} async-done(((bf16[256,1024]{1,0:T(8,128)(2,1)}), bf16[64,1024]{1,0:T(8,128)(2,1)}) %reduce-scatter.48.cloned.1.call-update) | async-done | bytes 131088 | tf_op jit(solution)/shard_map/reduce_scatter | solution.py:192
  723.8 22.6 %reduce-scatter.52.cloned.1.call-done = bf16[256,256]{1,0:T(8,128)(2,1)} async-done(((bf16[256,1024]{1,0:T(8,128)(2,1)}), bf16[256,256]{1,0:T(8,128)(2,1)}) %reduce-scatter.52.cloned.1.call-update) | async-done | bytes 131088 | tf_op jit(solution)/shard_map/reduce_scatter | solution.py:302
  748.1 28.8 %reduce-scatter.50.cloned.1.call-done = bf16[256,3,256]{2,0,1:T(8,128)(2,1)} async-done(((bf16[1024,3,256]{2,0,1:T(8,128)(2,1)}), bf16[256,3,256]{2,0,1:T(8,128)(2,1)}) %reduce-scatter.50.cloned.1.call-update) | async-done | bytes 393232 | tf_op jit(solution)/shard_map/reduce_scatter | solution.py:296
  778.8 31.7 %reduce-scatter.54.cloned.1.call-done = bf16[256,1024]{1,0:T(8,128)(2,1)} async-done(((bf16[1024,1024]{1,0:T(8,128)(2,1)}), bf16[256,1024]{1,0:T(8,128)(2,1)}) %reduce-scatter.54.cloned.1.call-update) | async-done | bytes 524304 | tf_op jit(solution)/shard_map/reduce_scatter | solution.py:305
  812.6 31.6 %reduce-scatter.56.cloned.1.call-done = bf16[1024,256]{1,0:T(8,128)(2,1)} async-done(((bf16[1024,1024]{1,0:T(8,128)(2,1)}), bf16[1024,256]{1,0:T(8,128)(2,1)}) %reduce-scatter.56.cloned.1.call-update) | async-done | bytes 524304 | tf_op jit(solution)/shard_map/reduce_scatter | solution.py:311
  (520 shorter events, 155.0 us)
Async XLA Ops:
  7.2 25.6 %copy-start.66 = (bf16[1,256,256]{2,1,0:T(8,128)(2,1)S(1)}, bf16[1,256,256]{2,1,0:T(8,128)(2,1)}, u32[]{:S(2)}) copy-start(bf16[1,256,256]{2,1,0:T(8,128)(2,1)} %param.20) | copy-start | bytes 393220
  7.2 34.3 %copy-start.135 = (s32[2,1,256]{2,1,0:T(1,128)S(1)}, s32[2,1,256]{2,1,0:T(1,128)}, u32[]{:S(2)}) copy-start(s32[2,1,256]{2,1,0:T(1,128)} %param.16) | copy-start | bytes 6148
  7.2 34.5 %all-gather.11.cloned.1.call-start = ((), (), s32[]{:S(2)}) async-start(), calls=%async_computation.35 | async-start | bytes 1966080 | tf_op jit(solution)/shard_map/all_gather | solution.py:242
  9.2 58.3 %reduce-scatter.26.cloned.1.call-start = ((), (), s32[]{:S(2)}) async-start(), calls=%async_computation.19 | async-start | bytes 655360 | tf_op jit(solution)/shard_map/reduce_scatter | solution.py:87
  41.4 78.3 %copy-start.97 = (s32[1,1,256]{2,1,0:T(1,128)}, s32[1,1,256]{2,1,0:T(1,128)S(1)}, u32[]{:S(2)}) copy-start(s32[1,1,256]{2,1,0:T(1,128)S(1)} %get-tuple-element.178) | copy-start | bytes 3076
  41.5 118.1 %copy-start.126 = (f32[3,256]{1,0:T(4,128)}, f32[3,256]{1,0:T(4,128)S(1)}, u32[]{:S(2)}) copy-start(f32[3,256]{1,0:T(4,128)S(1)} %pad_maximum_fusion.9) | copy-start | bytes 9220
  45.7 37.5 %copy-start.37 = (bf16[4,64,256]{2,1,0:T(8,128)(2,1)}, bf16[4,64,256]{2,1,0:T(8,128)(2,1)S(1)}, u32[]{:S(2)}) copy-start(bf16[4,64,256]{2,1,0:T(8,128)(2,1)S(1)} %convolution_convert_fusion.11) | copy-start | bytes 393220
  45.8 21.7 %copy-start = (bf16[2,1,64,1024]{3,2,1,0:T(8,128)(2,1)S(1)}, bf16[2,1,64,1024]{3,2,1,0:T(8,128)(2,1)}, u32[]{:S(2)}) copy-start(bf16[2,1,64,1024]{3,2,1,0:T(8,128)(2,1)} %param.15) | copy-start | bytes 786436
  47.0 45.0 %all-gather.13.cloned.1.call-start = ((), (), s32[]{:S(2)}) async-start(), calls=%async_computation.36 | async-start | bytes 2621440 | tf_op jit(solution)/shard_map/all_gather | solution.py:245
  47.7 68.5 %all-gather.15.cloned.1.call-start = ((), (), s32[]{:S(2)}) async-start(), calls=%async_computation.37 | async-start | bytes 2621440 | tf_op jit(solution)/shard_map/all_gather | solution.py:247
  48.3 91.4 %reduce-scatter.28.cloned.1.call-start = ((), (), s32[]{:S(2)}) async-start(), calls=%async_computation.20 | async-start | bytes 655360 | tf_op jit(solution)/shard_map/reduce_scatter | solution.py:103
  54.0 41.2 %copy-start.124 = (f32[1,2,4,128]{3,1,2,0:T(2,128)}, f32[1,2,4,128]{3,1,2,0:T(2,128)S(1)}, u32[]{:S(2)}) copy-start(f32[1,2,4,128]{3,1,2,0:T(2,128)S(1)} %copy.194) | copy-start | bytes 12292
  59.3 80.4 %copy-start.78 = (f32[1,1024]{1,0:T(1,128)}, f32[1,1024]{1,0:T(1,128)S(1)}, u32[]{:S(2)}) copy-start(f32[1,1024]{1,0:T(1,128)S(1)} %get-tuple-element.167) | copy-start | bytes 12292
  59.3 81.9 %copy-start.76 = (f32[1,1024]{1,0:T(1,128)}, f32[1,1024]{1,0:T(1,128)S(1)}, u32[]{:S(2)}) copy-start(f32[1,1024]{1,0:T(1,128)S(1)} %get-tuple-element.166) | copy-start | bytes 12292
  68.5 71.1 %copy-start.105 = (f32[64]{0:T(128)}, f32[64]{0:T(128)S(1)}, u32[]{:S(2)}) copy-start(f32[64]{0:T(128)S(1)} %broadcast_multiply_fusion.17) | copy-start | bytes 772
  69.7 25.6 %copy-start.127 = (f32[64]{0:T(128)}, f32[64]{0:T(128)S(1)}, u32[]{:S(2)}) copy-start(f32[64]{0:T(128)S(1)} %multiply_reduce_fusion.19) | copy-start | bytes 772
  69.7 70.0 %copy-start.115 = (f32[64]{0:T(128)}, f32[64]{0:T(128)S(1)}, u32[]{:S(2)}) copy-start(f32[64]{0:T(128)S(1)} %add_rsqrt_fusion.5) | copy-start | bytes 772
  95.2 44.4 %copy-start.12 = (bf16[64,1024]{1,0:T(8,128)(2,1)S(1)}, bf16[64,1024]{1,0:T(8,128)(2,1)}, u32[]{:S(2)}) copy-start(bf16[64,1024]{1,0:T(8,128)(2,1)} %reduce-scatter.26.cloned.1.call-done) | copy-start | bytes 393220
  119.7 70.5 %reduce-scatter.30.cloned.1.call-start = ((), (), s32[]{:S(2)}) async-start(), calls=%async_computation.21 | async-start | bytes 655360 | tf_op jit(solution)/shard_map/reduce_scatter | solution.py:87
  141.3 5.0 collective-permute-start
  164.8 27.6 %copy-start.38 = (bf16[4,64,256]{2,1,0:T(8,128)(2,1)}, bf16[4,64,256]{2,1,0:T(8,128)(2,1)S(1)}, u32[]{:S(2)}) copy-start(bf16[4,64,256]{2,1,0:T(8,128)(2,1)S(1)} %convolution_convert_fusion.10) | copy-start | bytes 393220
  164.8 41.1 %copy-start.125 = (f32[1,2,4,128]{3,1,2,0:T(2,128)S(1)}, f32[1,2,4,128]{3,1,2,0:T(2,128)}, u32[]{:S(2)}) copy-start(f32[1,2,4,128]{3,1,2,0:T(2,128)} %copy-done.124) | copy-start | bytes 12292
  166.0 69.6 %reduce-scatter.32.cloned.1.call-start = ((), (), s32[]{:S(2)}) async-start(), calls=%async_computation.22 | async-start | bytes 655360 | tf_op jit(solution)/shard_map/reduce_scatter | solution.py:103
  209.4 26.2 %copy-start.11 = (bf16[64,1024]{1,0:T(8,128)(2,1)S(1)}, bf16[64,1024]{1,0:T(8,128)(2,1)}, u32[]{:S(2)}) copy-start(bf16[64,1024]{1,0:T(8,128)(2,1)} %reduce-scatter.30.cloned.1.call-done) | copy-start | bytes 393220
  212.2 30.7 %copy-start.26 = (bf16[2,1,64,1024]{3,2,1,0:T(8,128)(2,1)S(1)}, bf16[2,1,64,1024]{3,2,1,0:T(8,128)(2,1)}, u32[]{:S(2)}) copy-start(bf16[2,1,64,1024]{3,2,1,0:T(8,128)(2,1)} %param.17) | copy-start | bytes 786436
  212.2 85.3 %reduce-scatter.34.cloned.1.call-start = ((), (), s32[]{:S(2)}) async-start(), calls=%async_computation.23 | async-start | bytes 655360 | tf_op jit(solution)/shard_map/reduce_scatter | solution.py:87
  235.6 23.0 %copy-start.150 = (bf16[1,1024,3,256]{1,3,2,0:T(8,128)(2,1)S(1)}, bf16[1,1024,3,256]{1,3,2,0:T(8,128)(2,1)}, u32[]{:S(2)}) copy-start(bf16[1,1024,3,256]{1,3,2,0:T(8,128)(2,1)} %all-gather.11.cloned.1.call-done) | copy-start | bytes 4718596
  239.8 5.8 collective-permute-start.1
  271.4 51.5 %reduce-scatter.38.cloned.1.call-start = ((), (), s32[]{:S(2)}) async-start(), calls=%async_computation.25 | async-start | bytes 655360 | tf_op jit(solution)/shard_map/reduce_scatter | solution.py:155
  292.5 30.4 %copy-start.13 = (bf16[64,1024]{1,0:T(8,128)(2,1)S(1)}, bf16[64,1024]{1,0:T(8,128)(2,1)}, u32[]{:S(2)}) copy-start(bf16[64,1024]{1,0:T(8,128)(2,1)} %reduce-scatter.26.cloned.1.call-done) | copy-start | bytes 393220
  294.1 72.3 %reduce-scatter.36.cloned.1.call-start = ((), (), s32[]{:S(2)}) async-start(), calls=%async_computation.24 | async-start | bytes 655360 | tf_op jit(solution)/shard_map/reduce_scatter | solution.py:103
  298.6 24.2 %copy-start.101 = (f32[64]{0:T(128)}, f32[64]{0:T(128)S(1)}, u32[]{:S(2)}) copy-start(f32[64]{0:T(128)S(1)} %broadcast_multiply_fusion.13) | copy-start | bytes 772
  343.1 83.7 %reduce-scatter.40.cloned.1.call-start = ((), (), s32[]{:S(2)}) async-start(), calls=%async_computation.26 | async-start | bytes 655360 | tf_op jit(solution)/shard_map/reduce_scatter | solution.py:192
  400.4 33.3 %copy-start.107 = (f32[64]{0:T(128)S(1)}, f32[64]{0:T(128)}, u32[]{:S(2)}) copy-start(f32[64]{0:T(128)} %copy-done.106) | copy-start | bytes 772
  403.5 75.4 %reduce-scatter.42.cloned.1.call-start = ((), (), s32[]{:S(2)}) async-start(), calls=%async_computation.27 | async-start | bytes 655360 | tf_op jit(solution)/shard_map/reduce_scatter | solution.py:155
  426.8 23.9 %copy-start.17 = (f32[256,1024]{1,0:T(8,128)S(1)}, f32[256,1024]{1,0:T(8,128)}, u32[]{:S(2)}) copy-start(f32[256,1024]{1,0:T(8,128)} %copy-done.16) | copy-start | bytes 3145732
  426.8 23.9 %copy-start.24 = (f32[256,1024]{1,0:T(8,128)S(1)}, f32[256,1024]{1,0:T(8,128)}, u32[]{:S(2)}) copy-start(f32[256,1024]{1,0:T(8,128)} %fusion.81) | copy-start | bytes 3145732
  428.0 5.7 collective-permute-start.2
  456.6 22.3 %copy-start.14 = (bf16[64,1024]{1,0:T(8,128)(2,1)S(1)}, bf16[64,1024]{1,0:T(8,128)(2,1)}, u32[]{:S(2)}) copy-start(bf16[64,1024]{1,0:T(8,128)(2,1)} %reduce-scatter.26.cloned.1.call-done) | copy-start | bytes 393220
  456.6 22.3 %copy-start.15 = (bf16[64,1024]{1,0:T(8,128)(2,1)S(1)}, bf16[64,1024]{1,0:T(8,128)(2,1)}, u32[]{:S(2)}) copy-start(bf16[64,1024]{1,0:T(8,128)(2,1)} %reduce-scatter.34.cloned.1.call-done) | copy-start | bytes 393220
  456.6 22.3 %copy-start.102 = (f32[64]{0:T(128)S(1)}, f32[64]{0:T(128)}, u32[]{:S(2)}) copy-start(f32[64]{0:T(128)} %copy-done.101) | copy-start | bytes 772
  456.6 82.7 %reduce-scatter.44.cloned.1.call-start = ((), (), s32[]{:S(2)}) async-start(), calls=%async_computation.28 | async-start | bytes 655360 | tf_op jit(solution)/shard_map/reduce_scatter | solution.py:192
  509.5 31.6 %copy-start.55 = (bf16[256,1,256]{2,0,1:T(8,128)(2,1)}, bf16[256,1,256]{2,0,1:T(8,128)(2,1)S(1)}, u32[]{:S(2)}) copy-start(bf16[256,1,256]{2,0,1:T(8,128)(2,1)S(1)} %copy.147) | copy-start | bytes 393220
  509.6 29.8 %copy-start.21 = (f32[64,1024]{1,0:T(8,128)S(1)}, f32[64,1024]{1,0:T(8,128)}, u32[]{:S(2)}) copy-start(f32[64,1024]{1,0:T(8,128)} %copy-done.20) | copy-start | bytes 786436
  512.9 34.1 %copy-start.111 = (f32[64]{0:T(128)S(1)}, f32[64]{0:T(128)}, u32[]{:S(2)}) copy-start(f32[64]{0:T(128)} %copy-done.110) | copy-start | bytes 772
  515.9 76.0 %reduce-scatter.46.cloned.1.call-start = ((), (), s32[]{:S(2)}) async-start(), calls=%async_computation.29 | async-start | bytes 655360 | tf_op jit(solution)/shard_map/reduce_scatter | solution.py:155
  541.2 5.9 collective-permute-start.3
  569.6 77.0 %reduce-scatter.62.cloned.1.call-start = ((), (), s32[]{:S(2)}) async-start(), calls=%async_computation.40 | async-start | bytes 81920
  570.4 21.5 %copy-start.100 = (f32[64]{0:T(128)S(1)}, f32[64]{0:T(128)}, u32[]{:S(2)}) copy-start(f32[64]{0:T(128)} %copy-done.99) | copy-start | bytes 772
  570.4 21.5 %copy-start.103 = (f32[64]{0:T(128)S(1)}, f32[64]{0:T(128)}, u32[]{:S(2)}) copy-start(f32[64]{0:T(128)} %copy-done.101) | copy-start | bytes 772
  570.4 21.5 %copy-start.104 = (f32[64]{0:T(128)S(1)}, f32[64]{0:T(128)}, u32[]{:S(2)}) copy-start(f32[64]{0:T(128)} %get-tuple-element.181) | copy-start | bytes 772
  570.4 21.5 %copy-start.109 = (f32[64]{0:T(128)S(1)}, f32[64]{0:T(128)}, u32[]{:S(2)}) copy-start(f32[64]{0:T(128)} %copy-done.108) | copy-start | bytes 772
  571.2 22.4 %copy-start.79 = (pred[256,256]{0,1:T(8,128)(4,1)}, pred[256,256]{0,1:T(8,128)(4,1)S(1)}, u32[]{:S(2)}) copy-start(pred[256,256]{0,1:T(8,128)(4,1)S(1)} %broadcast_compare_fusion) | copy-start | bytes 196612
  576.4 71.6 %reduce-scatter.58.cloned.1.call-start = ((), (), s32[]{:S(2)}) async-start(), calls=%async_computation.38 | async-start | bytes 20480
  617.7 80.3 %reduce-scatter.60.cloned.1.call-start = ((), (), s32[]{:S(2)}) async-start(), calls=%async_computation.39 | async-start | bytes 557056
  621.2 100.8 %reduce-scatter.48.cloned.1.call-start = ((), (), s32[]{:S(2)}) async-start(), calls=%async_computation.30 | async-start | bytes 655360 | tf_op jit(solution)/shard_map/reduce_scatter | solution.py:192
  624.3 122.1 %reduce-scatter.52.cloned.1.call-start = ((), (), s32[]{:S(2)}) async-start(), calls=%async_computation.32 | async-start | bytes 655360 | tf_op jit(solution)/shard_map/reduce_scatter | solution.py:302
  628.1 148.7 %reduce-scatter.50.cloned.1.call-start = ((), (), s32[]{:S(2)}) async-start(), calls=%async_computation.31 | async-start | bytes 1966080 | tf_op jit(solution)/shard_map/reduce_scatter | solution.py:296
  632.1 178.4 %reduce-scatter.54.cloned.1.call-start = ((), (), s32[]{:S(2)}) async-start(), calls=%async_computation.33 | async-start | bytes 2621440 | tf_op jit(solution)/shard_map/reduce_scatter | solution.py:305
  636.5 207.7 %reduce-scatter.56.cloned.1.call-start = ((), (), s32[]{:S(2)}) async-start(), calls=%async_computation.34 | async-start | bytes 2621440 | tf_op jit(solution)/shard_map/reduce_scatter | solution.py:311
  644.8 77.1 %copy-start.23 = (f32[64,1024]{1,0:T(8,128)S(1)}, f32[64,1024]{1,0:T(8,128)}, u32[]{:S(2)}) copy-start(f32[64,1024]{1,0:T(8,128)} %copy-done.22) | copy-start | bytes 786436
  644.9 77.1 %copy-start.29 = (f32[64,1024]{1,0:T(8,128)S(1)}, f32[64,1024]{1,0:T(8,128)}, u32[]{:S(2)}) copy-start(f32[64,1024]{1,0:T(8,128)} %copy-done.28) | copy-start | bytes 786436
  644.9 77.1 %copy-start.62 = (bf16[64,1024]{1,0:T(8,128)(2,1)S(1)}, bf16[64,1024]{1,0:T(8,128)(2,1)}, u32[]{:S(2)}) copy-start(bf16[64,1024]{1,0:T(8,128)(2,1)} %reduce-scatter.44.cloned.1.call-done) | copy-start | bytes 393220
  644.9 78.1 %copy-start.40 = (f32[1,64,1024]{2,1,0:T(8,128)S(1)}, f32[1,64,1024]{2,1,0:T(8,128)}, u32[]{:S(2)}) copy-start(f32[1,64,1024]{2,1,0:T(8,128)} %get-tuple-element.122) | copy-start | bytes 786436
  (116 other events, 567.8 us)
Sparse Core Ops, SparseCore 0:
  10.1 22.2 all-gather.10
  47.1 20.3 reduce-scatter.25
  69.0 22.8 all-gather.12
  93.4 22.8 all-gather.14
  119.8 19.7 reduce-scatter.27
  166.1 24.0 reduce-scatter.29
  212.4 23.1 reduce-scatter.31
  271.5 26.0 reduce-scatter.33
  300.4 22.3 reduce-scatter.37
  343.2 23.1 reduce-scatter.35
  403.6 23.1 reduce-scatter.39
  456.8 22.0 reduce-scatter.41
  516.0 23.2 reduce-scatter.43
  569.7 22.1 reduce-scatter.45
  594.1 19.0 reduce-scatter.61
  617.8 21.9 reduce-scatter.57
  643.2 54.7 reduce-scatter.59
  700.7 21.2 reduce-scatter.47
  725.0 21.3 reduce-scatter.51
  748.8 27.9 reduce-scatter.49
  779.4 31.1 reduce-scatter.53
  813.0 31.1 reduce-scatter.55
where the time goes:
time: 864 us; the launch traced here: 854 us
  waiting for transfers between devices  416 us (48%)
  blocking collectives  183 us (21%)
  matrix products  125 us (14%)
  other arithmetic  63.8 us (7%)
  local copies, waits for them, and re-layouts  39 us (5%)
  between operations  16.4 us (2%)
  starting transfers between devices  10.2 us (1%)
    reduce_scatter x3, waiting for transfers between devices, layer_backward(): lax.psum_scatter(jnp.einsum('tjn,cjn->tc', grad_qkv, qkv_mat, preferred_e...  64.3 us
    reduce_scatter x3, waiting for transfers between devices, layer_forward(): lax.psum_scatter(jnp.dot(activated, down_mat, preferred_element_type=jnp....  58.5 us
    reduce_scatter x3, waiting for transfers between devices, layer_backward(): lax.psum_scatter(jnp.dot(grad_pre_held, up_mat.T, preferred_element_type=...  53.3 us
    unnamed x25, waiting for transfers between devices  50.1 us
    all_gather x3, blocking collectives, layer_backward(): lax.all_gather(grad_two.astype(jnp.bfloat16), 'tensor', axis=0, tiled=True)  41.9 us
    all_gather x3, blocking collectives, layer_forward(): gathered = lax.all_gather(local_rows, 'tensor', axis=0, tiled=True)  41.4 us
    all_gather x3, blocking collectives, layer_forward(): lax.all_gather(hidden_one.astype(jnp.bfloat16), 'tensor', axis=0, tiled=T...  37.3 us
    all_gather x3, blocking collectives, layer_backward(): lax.all_gather(grad_one.astype(jnp.bfloat16), 'tensor', axis=0, tiled=True)  37.3 us
  transfers between devices with their start and end apart: 26, of which 22 were waited for; matrix products, arithmetic and copies ran while one was open for 11% of the time, Pallas kernels for 0%

commit v1 on v0

v1 whole, which is shorter than its diff:
```python
import functools

import jax
import jax.numpy as jnp
from jax import lax
from jax.experimental import pallas as pl
from jax.experimental.pallas import tpu as pltpu
from jax.sharding import PartitionSpec as P

MESH = pl.DeviceIdType.MESH
F32 = jnp.float32
BF16 = jnp.bfloat16
VMEM_SPEC = pl.BlockSpec(memory_space=pltpu.VMEM)
VMEM_LIMIT = 60 * 1024 * 1024


def line_barrier(me, count):
    barrier = pltpu.get_barrier_semaphore()

    @pl.when(me > 0)
    def _():
        pl.semaphore_signal(barrier, inc=1, device_id={"tensor": me - 1}, device_id_type=MESH)

    @pl.when(me < count - 1)
    def _():
        pl.semaphore_signal(barrier, inc=1, device_id={"tensor": me + 1}, device_id_type=MESH)

    inner = jnp.logical_and(me > 0, me < count - 1)

    @pl.when(inner)
    def _():
        pl.semaphore_wait(barrier, 2)

    @pl.when(jnp.logical_not(inner))
    def _():
        pl.semaphore_wait(barrier, 1)


def gather_kernel(count, own_ref, all_ref, send_sem, recv_sem):
    me = lax.axis_index("tensor")
    line_barrier(me, count)

    def copy_of(side, step):
        shard = me - step if side == 0 else me + step
        target = me + 1 if side == 0 else me - 1
        return pltpu.make_async_remote_copy(
            src_ref=own_ref if step == 0 else all_ref.at[shard],
            dst_ref=all_ref.at[shard],
            send_sem=send_sem.at[side, step],
            recv_sem=recv_sem.at[side, step],
            device_id={"tensor": target},
            device_id_type=MESH,
        )

    def arrival(side, step):
        shard = me - step if side == 0 else me + step
        return pltpu.make_async_remote_copy(
            src_ref=all_ref.at[shard],
            dst_ref=all_ref.at[shard],
            send_sem=send_sem.at[side, step - 1],
            recv_sem=recv_sem.at[side, step - 1],
            device_id={"tensor": me - 1 if side == 0 else me + 1},
            device_id_type=MESH,
        )

    def holds(side, step):
        return me >= step if side == 0 else me + step <= count - 1

    def sends(side):
        return me < count - 1 if side == 0 else me > 0

    for step in range(count):
        for side in range(2):

            @pl.when(holds(side, step))
            def _():
                if step > 0:
                    arrival(side, step).wait_recv()
                if step < count - 1:

                    @pl.when(sends(side))
                    def _():
                        copy_of(side, step).start()

        if step == 0:
            all_ref[me] = own_ref[...]
    for step in range(count - 1):
        for side in range(2):

            @pl.when(holds(side, step))
            def _():
                @pl.when(sends(side))
                def _():
                    copy_of(side, step).wait_send()


def tensor_gather(rows):
    count = lax.axis_size("tensor")
    gathered = pl.pallas_call(
        functools.partial(gather_kernel, count),
        out_shape=jax.ShapeDtypeStruct((count,) + rows.shape, rows.dtype),
        in_specs=[VMEM_SPEC],
        out_specs=VMEM_SPEC,
        scratch_shapes=[
            pltpu.SemaphoreType.DMA((2, count - 1)),
            pltpu.SemaphoreType.DMA((2, count - 1)),
        ],
        compiler_params=pltpu.CompilerParams(collective_id=1, has_side_effects=True),
        name="tensor_gather",
    )(rows)
    return gathered.reshape(count * rows.shape[0], rows.shape[1])


def scatter_kernel(count, part_ref, sum_ref, landed, staged, send_sem, recv_sem):
    me = lax.axis_index("tensor")
    line_barrier(me, count)

    def copy_of(side, slot, first, dest):
        return pltpu.make_async_remote_copy(
            src_ref=part_ref.at[dest] if first else staged.at[side, slot],
            dst_ref=landed.at[side, slot],
            send_sem=send_sem.at[side, slot],
            recv_sem=recv_sem.at[side, slot],
            device_id={"tensor": me + 1 if side == 0 else me - 1},
            device_id_type=MESH,
        )

    def roles(side, slot):
        dest = count - 1 - slot if side == 0 else slot
        passes = me < dest if side == 0 else me > dest
        first = me == 0 if side == 0 else me == count - 1
        return dest, passes, first

    for slot in range(count - 1):
        for side in range(2):
            dest, passes, first = roles(side, slot)

            @pl.when(first)
            def _():
                copy_of(side, slot, True, dest).start()

    for slot in range(count - 1):
        for side in range(2):
            dest, passes, first = roles(side, slot)

            @pl.when(jnp.logical_and(passes, jnp.logical_not(first)))
            def _():
                copy_of(side, slot, False, dest).wait_recv()
                staged[side, slot] = (
                    part_ref[dest].astype(F32) + landed[side, slot].astype(F32)
                ).astype(BF16)
                copy_of(side, slot, False, dest).start()

    for place in range(count):

        @pl.when(me == place)
        def _():
            total = part_ref[place].astype(F32)
            if place > 0:
                copy_of(0, count - 1 - place, False, place).wait_recv()
                total = total + landed[0, count - 1 - place].astype(F32)
            if place < count - 1:
                copy_of(1, place, False, place).wait_recv()
                total = total + landed[1, place].astype(F32)
            sum_ref[...] = total

    for slot in range(count - 1):
        for side in range(2):
            dest, passes, first = roles(side, slot)

            @pl.when(passes)
            def _():
                copy_of(side, slot, False, dest).wait_send()


def tensor_scatter(parts):
    count = lax.axis_size("tensor")
    rows = parts.shape[0] // count
    width = parts.shape[1]
    return pl.pallas_call(
        functools.partial(scatter_kernel, count),
        out_shape=jax.ShapeDtypeStruct((rows, width), F32),
        in_specs=[VMEM_SPEC],
        out_specs=VMEM_SPEC,
        scratch_shapes=[
            pltpu.VMEM((2, count - 1, rows, width), BF16),
            pltpu.VMEM((2, count - 1, rows, width), BF16),
            pltpu.SemaphoreType.DMA((2, count - 1)),
            pltpu.SemaphoreType.DMA((2, count - 1)),
        ],
        compiler_params=pltpu.CompilerParams(collective_id=2, has_side_effects=True),
        name="tensor_scatter",
    )(parts.reshape(count, rows, width))


class Cube:
    def __init__(self, dp_count):
        self.dp_count = dp_count
        self.dp_bits = dp_count.bit_length() - 1
        self.bits = self.dp_bits + 1
        self.size = 2 * dp_count
        self.section = lax.axis_index("section")
        self.dp = lax.axis_index("dp")

    def place(self, mask):
        section = 1 - self.section if mask & self.dp_count else self.section
        dp = self.dp
        for bit in range(self.dp_bits):
            if mask & (1 << bit):
                dp = dp + (1 << bit) * (1 - 2 * ((self.dp // (1 << bit)) % 2))
        return section, dp

    def device(self, mask):
        section, dp = self.place(mask)
        return {"section": section, "dp": dp}

    def order(self, kind):
        bits = list(range(self.bits - 1, -1, -1))
        if kind:
            bits[0], bits[1] = bits[1], bits[0]
        return bits

    def greet(self, others=()):
        barrier = pltpu.get_barrier_semaphore()
        targets = [self.device(1 << bit) for bit in range(self.bits)] + list(others)
        for target in targets:
            pl.semaphore_signal(barrier, inc=1, device_id=target, device_id_type=MESH)
        pl.semaphore_wait(barrier, len(targets))


def block_of(ref, form, place, shape, half):
    section, dp = place
    if form == "rows":
        rows = shape[-2]
        at = pl.ds(pl.multiple_of(dp * rows, rows), rows)
        return (section, slice(None), at) if len(shape) == 3 else (section, at)
    if form == "columns":
        low, high = half
        return (
            section,
            pl.ds(low, high - low),
            pl.ds(pl.multiple_of(dp * shape[-1], shape[-1]), shape[-1]),
        )
    if len(shape) == 2 and half is not None:
        return (section, dp, pl.ds(half[0], half[1] - half[0]))
    return (section, dp)


def weights_kernel(pieces, count, dp_count, *refs):
    own = refs[:count]
    full = refs[count : 2 * count]
    send_sem, recv_sem, local_sem = refs[2 * count :]
    cube = Cube(dp_count)
    cube.greet()

    def source(piece):
        which, form, shape, half, kind = piece
        return own[which] if half is None else own[which].at[pl.ds(half[0], half[1] - half[0])]

    def slot(piece, mask):
        which, form, shape, half, kind = piece
        return full[which].at[block_of(full[which], form, cube.place(mask), shape, half)]

    def copy_of(number, piece, mask, bit, receiving=False):
        held = mask if receiving else mask ^ (1 << bit)
        return pltpu.make_async_remote_copy(
            src_ref=source(piece) if held == 0 else slot(piece, held),
            dst_ref=slot(piece, held),
            send_sem=send_sem.at[number, mask],
            recv_sem=recv_sem.at[number, mask],
            device_id=cube.device(1 << bit),
            device_id_type=MESH,
        )

    def steps(piece):
        order = cube.order(piece[4])
        held = [0]
        out = []
        for bit in order:
            fresh = [mask | (1 << bit) for mask in held]
            out += [(mask, bit) for mask in fresh]
            held = held + fresh
        return out

    locals_ = []
    for number, piece in enumerate(pieces):
        for mask, bit in steps(piece):
            if mask == 1 << bit:
                copy_of(number, piece, mask, bit).start()
    for number, piece in enumerate(pieces):
        copy = pltpu.make_async_copy(source(piece), slot(piece, 0), local_sem.at[number])
        copy.start()
        locals_.append(copy)
    rounds = cube.size
    waited = [set() for _ in pieces]
    for turn in range(rounds):
        for number, piece in enumerate(pieces):
            relays = [(m, b) for m, b in steps(piece)]
            landing = [m for m, b in relays]
            if turn >= len(landing):
                continue
            mask = landing[turn]
            bit_in = dict(relays)[mask]
            copy_of(number, piece, mask, bit_in, True).wait_recv()
            for later, bit in relays:
                if later ^ (1 << bit) == mask and later != 1 << bit:
                    copy_of(number, piece, later, bit).start()
    for number, piece in enumerate(pieces):
        for mask, bit in steps(piece):
            copy_of(number, piece, mask, bit).wait_send()
    for copy in locals_:
        copy.wait()


def full_shape(form, shape, dp_count):
    if form == "rows":
        return (2,) + shape[:-2] + (dp_count * shape[-2], shape[-1])
    if form == "columns":
        return (2, shape[0], dp_count * shape[1])
    return (2, dp_count) + shape


def pieces_of(forms, shapes):
    pieces = []
    for which, (form, shape) in enumerate(zip(forms, shapes)):
        if which == 3:
            middle = shape[0] // 2
            pieces.append((which, form, shape, (0, middle), 0))
            pieces.append((which, form, shape, (middle, shape[0]), 1))
        elif which == 1:
            pieces.append((which, form, shape, (0, shape[0]), 0))
        else:
            pieces.append((which, form, shape, None, 1 if which == 2 else 0))
    return pieces


def gather_weights(arrays, forms):
    dp_count = lax.axis_size("dp")
    shapes = [array.shape for array in arrays]
    pieces = pieces_of(forms, shapes)
    count = len(arrays)
    return pl.pallas_call(
        functools.partial(weights_kernel, pieces, count, dp_count),
        out_shape=[
            jax.ShapeDtypeStruct(full_shape(form, shape, dp_count), BF16)
            for form, shape in zip(forms, shapes)
        ],
        in_specs=[VMEM_SPEC] * count,
        out_specs=[VMEM_SPEC] * count,
        scratch_shapes=[
            pltpu.SemaphoreType.DMA((len(pieces), 2 * dp_count)),
            pltpu.SemaphoreType.DMA((len(pieces), 2 * dp_count)),
            pltpu.SemaphoreType.DMA((len(pieces),)),
        ],
        compiler_params=pltpu.CompilerParams(
            collective_id=3, has_side_effects=True, vmem_limit_bytes=VMEM_LIMIT
        ),
        name="gather_weights",
    )(*arrays)


def piece_shape(piece):
    which, form, shape, half, kind = piece
    return shape if half is None else (half[1] - half[0],) + shape[1:]


def grads_kernel(pieces, count, dp_count, line, *refs):
    parts = refs[:count]
    sums = refs[count : 2 * count]
    row_sum = refs[2 * count]
    landed = refs[2 * count + 1 : 2 * count + 1 + len(pieces)]
    line_buf, send_sem, recv_sem, line_send, line_recv = refs[2 * count + 1 + len(pieces) :]
    cube = Cube(dp_count)
    here = lax.axis_index("tensor")
    others = [{"tensor": lax.rem(here + step, line)} for step in range(1, line)]
    cube.greet(others)

    def part(piece, mask):
        which, form, shape, half, kind = piece
        return parts[which].at[block_of(parts[which], form, cube.place(mask), shape, half)]

    def plan(piece):
        order = cube.order(piece[4])[::-1]
        active = list(range(cube.size))
        levels = []
        at = 0
        for bit in order:
            kept = [mask for mask in active if not mask & (1 << bit)]
            kept.sort(key=lambda mask: -sum(1 << order.index(b) for b in order if mask & (1 << b)))
            kept.sort(
                key=lambda mask: min(
                    [order.index(b) for b in order if mask & (1 << b)] + [len(order)]
                )
            )
            levels.append((bit, [(mask, at + i) for i, mask in enumerate(kept)]))
            at += len(kept)
            active = kept
        return levels

    plans = [plan(piece) for piece in pieces]

    def slot_of(number, level, mask):
        return dict(plans[number][level][1])[mask]

    def copy_of(number, level, mask):
        piece = pieces[number]
        bit = plans[number][level][0]
        slot = slot_of(number, level, mask)
        sent = mask | (1 << bit)
        return pltpu.make_async_remote_copy(
            src_ref=part(piece, sent)
            if level == 0
            else landed[number].at[slot_of(number, level - 1, sent)],
            dst_ref=landed[number].at[slot],
            send_sem=send_sem.at[number, slot],
            recv_sem=recv_sem.at[number, slot],
            device_id=cube.device(1 << bit),
            device_id_type=MESH,
        )

    for place in range(cube.size // 2):
        for number in range(len(pieces)):
            copy_of(number, 0, plans[number][0][1][place][0]).start()

    def fold(number, level, mask, final):
        piece = pieces[number]
        which, form, shape, half, kind = piece
        slot = slot_of(number, level, mask)
        full = piece_shape(piece)
        rows = full[-2]
        chunk = rows if rows <= 32 else 32
        base = (
            part(piece, mask)
            if level == 0
            else landed[number].at[slot_of(number, level - 1, mask)]
        )
        lead = (slice(None),) * (len(full) - 2)

        def one(index, carry):
            at = pl.ds(pl.multiple_of(index * chunk, chunk), chunk)
            total = base[lead + (at,)].astype(F32) + landed[number][(slot,) + lead + (at,)].astype(F32)
            if final:
                low = 0 if half is None else half[0]
                to = pl.ds(pl.multiple_of(low + index * chunk, chunk), chunk)
                sums[which][lead + (to,)] = total
            else:
                landed[number][(slot,) + lead + (at,)] = total.astype(landed[number].dtype)
            return carry

        if rows == chunk:
            one(0, 0)
        else:
            lax.fori_loop(0, rows // chunk, one, 0)

    depth = cube.bits
    for level in range(depth):
        masks = len(plans[0][level][1])
        for place in range(masks):
            for number in list(range(len(pieces)))[::-1]:
                mask = plans[number][level][1][place][0]
                copy_of(number, level, mask).wait_recv()
                final = level == depth - 1
                fold(number, level, mask, final)
                if not final:
                    bit_next = plans[number][level + 1][0]
                    if mask & (1 << bit_next):
                        copy_of(number, level + 1, mask ^ (1 << bit_next)).start()
                elif pieces[number][0] == count - 1:
                    for step in range(1, line):
                        line_copy(step, others, sums[count - 1], line_buf, line_send, line_recv).start()
    total = sums[count - 1][...]
    for step in range(1, line):
        line_copy(step, others, sums[count - 1], line_buf, line_send, line_recv).wait_recv()
        total = total + line_buf[step - 1]
    row_sum[...] = total
    for step in range(1, line):
        line_copy(step, others, sums[count - 1], line_buf, line_send, line_recv).wait_send()
    for number in range(len(pieces)):
        for level in range(depth):
            for mask, slot in plans[number][level][1]:
                copy_of(number, level, mask).wait_send()


def line_copy(step, others, source, line_buf, line_send, line_recv):
    return pltpu.make_async_remote_copy(
        src_ref=source,
        dst_ref=line_buf.at[step - 1],
        send_sem=line_send.at[step - 1],
        recv_sem=line_recv.at[step - 1],
        device_id=others[step - 1],
        device_id_type=MESH,
    )


def scatter_grads(arrays, forms, shapes):
    dp_count = lax.axis_size("dp")
    line = lax.axis_size("tensor")
    pieces = pieces_of(forms, shapes)
    count = len(arrays)
    slots = 2 * dp_count - 1
    return pl.pallas_call(
        functools.partial(grads_kernel, pieces, count, dp_count, line),
        out_shape=[jax.ShapeDtypeStruct(shape, F32) for shape in shapes]
        + [jax.ShapeDtypeStruct(shapes[-1], F32)],
        in_specs=[VMEM_SPEC] * count,
        out_specs=[VMEM_SPEC] * (count + 1),
        scratch_shapes=[
            pltpu.VMEM((slots,) + piece_shape(piece), arrays[piece[0]].dtype) for piece in pieces
        ]
        + [
            pltpu.VMEM((line - 1,) + shapes[-1], F32),
            pltpu.SemaphoreType.DMA((len(pieces), slots)),
            pltpu.SemaphoreType.DMA((len(pieces), slots)),
            pltpu.SemaphoreType.DMA((line - 1,)),
            pltpu.SemaphoreType.DMA((line - 1,)),
        ],
        compiler_params=pltpu.CompilerParams(
            collective_id=4, has_side_effects=True, vmem_limit_bytes=VMEM_LIMIT
        ),
        name="scatter_grads",
    )(*arrays)


def gelu_exact(values):
    return 0.5 * values * (1.0 + jax.scipy.special.erf(values * 0.7071067811865476))


def gelu_slope(values):
    return (
        0.5 * (1.0 + jax.scipy.special.erf(values * 0.7071067811865476))
        + values * jnp.exp(-0.5 * values * values) * 0.3989422804014327
    )


def normalize(summed):
    center = summed - jnp.mean(summed, axis=-1, keepdims=True)
    scaled = lax.rsqrt(jnp.mean(center * center, axis=-1, keepdims=True) + 1e-12)
    return (center * scaled, scaled)


def norm_back(upstream, normed, scaled):
    return scaled * (
        upstream
        - jnp.mean(upstream, axis=-1, keepdims=True)
        - normed * jnp.mean(upstream * normed, axis=-1, keepdims=True)
    )


def masked_probs(queries, keys, same_seq):
    scores = jnp.einsum(
        "qhd,khd->hqk", queries, keys, preferred_element_type=jnp.float32
    ) * queries.shape[2] ** (-0.5)
    scores = jnp.where(same_seq[None], scores, -jnp.inf)
    largest = jnp.max(scores, axis=-1, keepdims=True)
    shifted = jnp.exp(scores - largest)
    return shifted / jnp.sum(shifted, axis=-1, keepdims=True)


def split_heads(qkv_held, which, head_count, head_size):
    return qkv_held[:, which].reshape(qkv_held.shape[0], head_count, head_size)


def layer_forward(local_rows, pack_ids, weights):
    qkv_mat, qv_shift, out_mat, up_mat, up_shift, down_mat, row_params = weights
    gathered = tensor_gather(local_rows)
    tokens = gathered.shape[0]
    width = qkv_mat.shape[2]
    head_count = qv_shift.shape[1]
    head_size = qv_shift.shape[2]
    projected = jnp.einsum("tc,jcn->tjn", gathered, qkv_mat, preferred_element_type=jnp.float32)
    qv_wide = qv_shift.astype(jnp.float32).reshape(2, width)
    bias_rows = jnp.concatenate(
        [qv_wide[0:1], jnp.zeros((1, width), jnp.float32), qv_wide[1:2]], axis=0
    )
    qkv_held = (projected + bias_rows[None]).astype(jnp.bfloat16)
    queries = split_heads(qkv_held, 0, head_count, head_size)
    keys = split_heads(qkv_held, 1, head_count, head_size)
    values = split_heads(qkv_held, 2, head_count, head_size)
    same_seq = pack_ids[:, None] == pack_ids[None, :]
    attn_prob = masked_probs(queries, keys, same_seq)
    context = (
        jnp.einsum(
            "hqk,khd->qhd",
            attn_prob.astype(jnp.bfloat16),
            values,
            preferred_element_type=jnp.float32,
        )
        .reshape(tokens, width)
        .astype(jnp.bfloat16)
    )
    params_wide = row_params.astype(jnp.float32)
    attn_part = tensor_scatter(jnp.dot(context, out_mat, preferred_element_type=jnp.float32).astype(jnp.bfloat16))
    resid_one = local_rows.astype(jnp.float32) + attn_part + params_wide[0]
    normed_one, scaled_one = normalize(resid_one)
    hidden_one = normed_one * params_wide[1] + params_wide[2]
    hidden_in = tensor_gather(hidden_one.astype(jnp.bfloat16))
    pre_act = jnp.dot(hidden_in, up_mat, preferred_element_type=jnp.float32) + up_shift.astype(
        jnp.float32
    ).reshape(-1)
    activated = gelu_exact(pre_act).astype(jnp.bfloat16)
    resid_two = (
        hidden_one
        + tensor_scatter(jnp.dot(activated, down_mat, preferred_element_type=jnp.float32).astype(jnp.bfloat16))
        + params_wide[3]
    )
    normed_two, scaled_two = normalize(resid_two)
    layer_out = (normed_two * params_wide[4] + params_wide[5]).astype(jnp.bfloat16)
    saved = (
        gathered,
        qkv_held,
        context,
        normed_one,
        scaled_one,
        hidden_in,
        pre_act,
        activated,
        normed_two,
        scaled_two,
    )
    return (layer_out, saved)


def layer_backward(upstream, pack_ids, weights, saved):
    qkv_mat, qv_shift, out_mat, up_mat, up_shift, down_mat, row_params = weights
    (
        gathered,
        qkv_held,
        context,
        normed_one,
        scaled_one,
        hidden_in,
        pre_act,
        activated,
        normed_two,
        scaled_two,
    ) = saved
    tokens = gathered.shape[0]
    width = qkv_mat.shape[2]
    head_count = qv_shift.shape[1]
    head_size = qv_shift.shape[2]
    params_wide = row_params.astype(jnp.float32)
    grad_two = norm_back(upstream * params_wide[4], normed_two, scaled_two)
    grad_full = tensor_gather(grad_two.astype(jnp.bfloat16))
    down_grad = jnp.dot(activated.T, grad_full, preferred_element_type=jnp.float32)
    grad_pre = jnp.dot(grad_full, down_mat.T, preferred_element_type=jnp.float32) * gelu_slope(
        pre_act
    )
    grad_pre_held = grad_pre.astype(jnp.bfloat16)
    up_grad = jnp.dot(hidden_in.T, grad_pre_held, preferred_element_type=jnp.float32)
    grad_hidden = grad_two + tensor_scatter(jnp.dot(grad_pre_held, up_mat.T, preferred_element_type=jnp.float32).astype(jnp.bfloat16))
    grad_one = norm_back(grad_hidden * params_wide[1], normed_one, scaled_one)
    resid_full = tensor_gather(grad_one.astype(jnp.bfloat16))
    out_grad = jnp.dot(context.T, resid_full, preferred_element_type=jnp.float32)
    grad_context = (
        jnp.dot(resid_full, out_mat.T, preferred_element_type=jnp.float32)
        .astype(jnp.bfloat16)
        .reshape(tokens, head_count, head_size)
    )
    queries = split_heads(qkv_held, 0, head_count, head_size)
    keys = split_heads(qkv_held, 1, head_count, head_size)
    values = split_heads(qkv_held, 2, head_count, head_size)
    same_seq = pack_ids[:, None] == pack_ids[None, :]
    attn_prob = masked_probs(queries, keys, same_seq)
    grad_prob = jnp.einsum("qhd,khd->hqk", grad_context, values, preferred_element_type=jnp.float32)
    row_dots = jnp.sum(attn_prob * grad_prob, axis=-1, keepdims=True)
    grad_scores = (attn_prob * (grad_prob - row_dots) * head_size ** (-0.5)).astype(jnp.bfloat16)
    grad_queries = jnp.einsum("hqk,khd->qhd", grad_scores, keys, preferred_element_type=jnp.float32)
    grad_keys = jnp.einsum("hqk,qhd->khd", grad_scores, queries, preferred_element_type=jnp.float32)
    grad_values = jnp.einsum(
        "hqk,qhd->khd",
        attn_prob.astype(jnp.bfloat16),
        grad_context,
        preferred_element_type=jnp.float32,
    )
    qv_grad = jnp.stack([jnp.sum(grad_queries, axis=0), jnp.sum(grad_values, axis=0)])
    grad_qkv = (
        jnp.stack([grad_queries, grad_keys, grad_values], axis=1)
        .reshape(tokens, 3, width)
        .astype(jnp.bfloat16)
    )
    qkv_grad = jnp.einsum("tc,tjn->jcn", gathered, grad_qkv, preferred_element_type=jnp.float32)
    grad_inputs = grad_one + tensor_scatter(jnp.einsum("tjn,jcn->tc", grad_qkv, qkv_mat, preferred_element_type=jnp.float32).astype(
            jnp.bfloat16
        ))
    row_grads = jnp.stack(
        [
            jnp.sum(grad_one, axis=0),
            jnp.sum(grad_hidden * normed_one, axis=0),
            jnp.sum(grad_hidden, axis=0),
            jnp.sum(grad_two, axis=0),
            jnp.sum(upstream * normed_two, axis=0),
            jnp.sum(upstream, axis=0),
        ]
    )
    up_shift_grad = jnp.sum(grad_pre, axis=0).reshape(up_shift.shape)
    return (
        grad_inputs,
        (qkv_grad, qv_grad, out_grad, up_grad, up_shift_grad, down_grad),
        row_grads,
    )


def shards(
    block_input,
    seq_ids,
    out_cotangent,
    qkv_weight,
    qv_bias,
    out_weight,
    out_bias,
    norm1_gain,
    norm1_bias,
    up_weight,
    up_bias,
    down_weight,
    down_bias,
    norm2_gain,
    norm2_bias,
):
    section = lax.axis_index("section")
    first = section == 0
    dp_count = lax.axis_size("dp")
    line = lax.axis_size("tensor")
    heads, head_part = qv_bias.shape[2], qv_bias.shape[3]
    groups, unit_part = up_bias.shape[1], up_bias.shape[2]
    part = out_bias.shape[1]
    columns = "columns" if part % 128 == 0 else "stack"
    forms = ["rows", columns, "rows", columns, "stack"]

    small_sizes = (qv_bias[0].size, up_bias[0].size, 6 * part)
    small_rows = -(-sum(small_sizes) // 2048) * 16
    small = jnp.concatenate(
        [
            qv_bias.reshape(-1),
            up_bias.reshape(-1),
            out_bias[0],
            norm1_gain[0],
            norm1_bias[0],
            down_bias[0],
            norm2_gain[0],
            norm2_bias[0],
            jnp.zeros((small_rows * 128 - sum(small_sizes),), BF16),
        ]
    ).reshape(small_rows, 128)
    stacked = gather_weights(
        (jnp.swapaxes(qkv_weight[0], 0, 1), out_weight[0], up_weight[0], down_weight[0], small),
        forms,
    )

    def layer_weights(which):
        qkv_full, out_full, up_full, down_full, small_full = [array[which] for array in stacked]
        if columns == "stack":
            out_full, down_full = [
                jnp.moveaxis(array, 0, 1).reshape(array.shape[1], -1)
                for array in (out_full, down_full)
            ]
        flat = small_full.reshape(dp_count, -1)
        qv_full = flat[:, : small_sizes[0]].reshape(dp_count, 2, heads, head_part)
        qv_full = jnp.moveaxis(qv_full, 0, 2).reshape(2, heads, dp_count * head_part)
        middle = small_sizes[0] + small_sizes[1]
        up_shift = flat[:, small_sizes[0] : middle].reshape(dp_count, groups, unit_part)
        up_shift = jnp.moveaxis(up_shift, 0, 1).reshape(groups, dp_count * unit_part)
        row_params = flat[:, middle : middle + small_sizes[2]].reshape(dp_count, 6, part)
        row_params = jnp.moveaxis(row_params, 0, 1).reshape(6, dp_count * part)
        return (qkv_full, qv_full, out_full, up_full, up_shift, down_full, row_params)

    weights = [layer_weights(0), layer_weights(1)]
    rows = jnp.where(first, block_input[0, 0], block_input[1, 0])
    ids = jnp.where(first, seq_ids[0, 0], seq_ids[1, 0])
    upstream = jnp.where(first, out_cotangent[0, 0], out_cotangent[1, 0]).astype(F32)
    out_first, saved_first = layer_forward(rows, ids, weights[0])
    out_last, saved_last = layer_forward(out_first, ids, weights[1])
    swap = [(0, 1), (1, 0)]
    other_out = lax.ppermute(jnp.where(first, out_last, out_first), "section", swap)
    own_out = jnp.where(first, out_first, out_last)
    section_outputs = jnp.stack(
        [jnp.where(first, own_out, other_out), jnp.where(first, other_out, own_out)]
    )
    grad_last, mats_last, rows_last = layer_backward(upstream, ids, weights[1], saved_last)
    grad_first, mats_first, rows_first = layer_backward(grad_last, ids, weights[0], saved_first)
    other_grad = lax.ppermute(
        jnp.where(first, grad_last, grad_first).astype(BF16), "section", swap
    ).astype(F32)
    own_grad = jnp.where(first, grad_first, grad_last)
    input_grads = jnp.stack(
        [jnp.where(first, own_grad, other_grad), jnp.where(first, other_grad, own_grad)]
    )

    def blocks(array):
        cut = array.reshape(array.shape[:-1] + (dp_count, array.shape[-1] // dp_count))
        return jnp.moveaxis(cut, -2, 0)

    def padded(flat):
        size = -(-flat.shape[1] // 1024) * 1024
        return jnp.pad(flat, ((0, 0), (0, size - flat.shape[1]))).reshape(dp_count, -1, 128)

    def packed(mats, row_grads):
        qkv_grad, qv_grad, out_grad, up_grad, up_shift_grad, down_grad = mats
        qv_flat = blocks(qv_grad.reshape(2, heads, -1)).reshape(dp_count, -1)
        up_flat = blocks(up_shift_grad).reshape(dp_count, -1)
        bias_flat = padded(jnp.concatenate([qv_flat, up_flat], axis=1))
        row_flat = padded(blocks(row_grads).reshape(dp_count, -1))
        if columns == "stack":
            out_grad, down_grad = blocks(out_grad), blocks(down_grad)
        return (
            qkv_grad.astype(BF16),
            out_grad.astype(BF16),
            up_grad.astype(BF16),
            down_grad.astype(BF16),
            bias_flat,
            row_flat,
        )

    both = [
        jnp.stack(pair) for pair in zip(packed(mats_first, rows_first), packed(mats_last, rows_last))
    ]
    shapes = [
        (3, part, qkv_weight.shape[3]),
        out_weight.shape[1:],
        up_weight.shape[1:],
        down_weight.shape[1:],
        both[4].shape[2:],
        both[5].shape[2:],
    ]
    qkv_sum, out_sum, up_sum, down_sum, bias_sum, _, row_sum = scatter_grads(
        both, forms + ["stack"], shapes
    )
    bias_sum = bias_sum.reshape(-1)
    qv_sum = bias_sum[: small_sizes[0]].reshape(1, 2, heads, head_part)
    up_shift_sum = bias_sum[small_sizes[0] : small_sizes[0] + small_sizes[1]].reshape(
        1, groups, unit_part
    )
    row_sum = row_sum.reshape(-1)[: 6 * part].reshape(6, line, part // line)
    row_sum = lax.dynamic_index_in_dim(row_sum, lax.axis_index("tensor"), 1, keepdims=False)
    return (
        section_outputs[None, :, None],
        input_grads[None, :, None],
        jnp.swapaxes(qkv_sum, 0, 1)[None],
        qv_sum,
        out_sum[None],
        row_sum[0][None],
        row_sum[1][None],
        row_sum[2][None],
        up_sum[None],
        up_shift_sum,
        down_sum[None],
        row_sum[3][None],
        row_sum[4][None],
        row_sum[5][None],
    )


def solution(mesh):
    return jax.shard_map(
        shards,
        mesh=mesh,
        in_specs=(
            P(None, "dp", "tensor", None),
            P(None, "dp", None),
            P(None, "dp", "tensor", None),
            P("section", "dp", None, "tensor"),
            P("section", None, "tensor", "dp"),
            P("section", "tensor", "dp"),
            P("section", "dp"),
            P("section", "dp"),
            P("section", "dp"),
            P("section", "dp", "tensor"),
            P("section", "tensor", "dp"),
            P("section", "tensor", "dp"),
            P("section", "dp"),
            P("section", "dp"),
            P("section", "dp"),
        ),
        out_specs=(
            P("section", None, "dp", "tensor", None),
            P("section", None, "dp", "tensor", None),
            P("section", "dp", None, "tensor"),
            P("section", None, "tensor", "dp"),
            P("section", "tensor", "dp"),
            P("section", ("dp", "tensor")),
            P("section", ("dp", "tensor")),
            P("section", ("dp", "tensor")),
            P("section", "dp", "tensor"),
            P("section", "tensor", "dp"),
            P("section", "tensor", "dp"),
            P("section", ("dp", "tensor")),
            P("section", ("dp", "tensor")),
            P("section", ("dp", "tensor")),
        ),
        check_vma=False,
    )
```

time: 864 us -> 542 us (0.63); the launches traced: 854 us -> 541 us
  waiting for transfers between devices: 416 us -> 0.01 us
  Pallas kernels: 0 us -> 404 us
  blocking collectives: 183 us -> 0 us
  matrix products: 125 us -> 69.1 us
  local copies, waits for them, and re-layouts: 39 us -> 18.5 us
  other arithmetic: 63.8 us -> 44.9 us
  between operations: 16.4 us -> 1.98 us
    pallas_call x0 -> x18, Pallas kernels: none -> 404 us  [the longest x8 120 us: tensor_scatter(): pl.pallas_call(functools.partial(scatter_kernel, count), out_shape=jax.Sh...]
    reduce_scatter x16 -> x0, waiting for transfers between devices: 327 us -> none  [the longest x3 64.3 us: layer_backward(): lax.psum_scatter(jnp.einsum('tjn,cjn->tc', grad_qkv, qkv_mat, preferred_e...]
    all_gather x16 -> x0, blocking collectives: 183 us -> none  [the longest x3 41.9 us: layer_backward(): lax.all_gather(grad_two.astype(jnp.bfloat16), 'tensor', axis=0, tiled=True)]
    unnamed x25 -> x0, waiting for transfers between devices: 50.1 us -> none
    all_gather x3 -> x0, waiting for transfers between devices: 29.8 us -> none  [the longest x1 21 us: shards(): lax.all_gather(down_weight[0], 'dp', axis=1, tiled=True)]
    unnamed x325 -> x193, local copies, waits for them, and re-layouts: 21.5 us -> 8.13 us
    another operation x4 -> x8, other arithmetic: 4.46 us -> 14.1 us  [the longest x6 12 us: shards(): jnp.stack(pair)]
    ppermute x4 -> x2, waiting for transfers between devices: 9.63 us -> 0.01 us  [the longest x1 0.01 us: shards(): lax.ppermute(jnp.where(first, out_last, out_first), 'section', swap)]
  transfers between devices with their start and end apart: 26 -> 2, of which waited for: 22 -> 0; matrix products, arithmetic and copies ran while one was open for 11% -> 15% of each run, Pallas kernels for 0% -> 42%
where the time goes in v1:
time: 542 us; the launch traced here: 541 us
  Pallas kernels  404 us (75%)
  matrix products  69.1 us (13%)
  other arithmetic  44.9 us (8%)
  local copies, waits for them, and re-layouts  18.5 us (3%)
    pallas_call x8, Pallas kernels, tensor_scatter(): pl.pallas_call(functools.partial(scatter_kernel, count), out_shape=jax.Sh...  120 us
    pallas_call x1, Pallas kernels, scatter_grads(): pl.pallas_call(functools.partial(grads_kernel, pieces, count, dp_count, l...  118 us
    pallas_call x8, Pallas kernels, tensor_gather(): pl.pallas_call(functools.partial(gather_kernel, count), out_shape=jax.Sha...  102 us
    pallas_call x1, Pallas kernels, gather_weights(): pl.pallas_call(functools.partial(weights_kernel, pieces, count, dp_count)...  64 us
    another operation x6, other arithmetic, shards(): jnp.stack(pair)  12 us
  transfers between devices with their start and end apart: 2, of which 0 were waited for; matrix products, arithmetic and copies ran while one was open for 15% of the time, Pallas kernels for 42%

profile of v1, /device:TPU:1, one launch (start us, length us, event | category | flops | bytes accessed | tf_op | source)
XLA Modules:
  0.0 540.8 jit_solution(14405472972325789342)
XLA Ops:
  8.8 64.0 %gather_weights.1 = (bf16[2,3,1024,256]{3,2,1,0:T(8,128)(2,1)}, bf16[2,256,1024]{2,1,0:T(8,128)(2,1)}, bf16[2,1024,1024]{2,1,0:T(8,128)(2,1)}, bf16[2,1024,1024]{2,1,0:T(8,128)(2,1)}, bf16[2,4,16,128]{3,2,1,0:T(8,128)(2,1)}) custom-call(bf16[3,256,256]{2,1,0:T(8,128)(2,1)} %bitcast.394, bf16[256,256]{1,0:T(8,128)(2,1)} %bitcast.402, ...), custom_call_target="tpu_custom_call" | custom-call | tf_op jit(solution)/shard_map/gather_weights/pallas_call | solution.py:342
  74.5 1.7 select_bitcast_fusion.2.own_ref
  76.2 14.7 %tensor_gather.8 = bf16[4,64,1024]{2,1,0:T(8,128)(2,1)} custom-call(bf16[64,1024]{1,0:T(8,128)(2,1)} %select_bitcast_fusion.2.own_ref), custom_call_target="tpu_custom_call" | custom-call | tf_op jit(solution)/shard_map/tensor_gather/pallas_call | solution.py:99
  92.0 2.4 fusion.101
  94.5 1.5 fusion.200
  96.8 1.1 convolution_convert_fusion.5
  97.9 15.0 %tensor_scatter.8 = f32[64,1024]{1,0:T(8,128)} custom-call(bf16[4,64,1024]{2,1,0:T(8,128)(2,1)} %bitcast.373), custom_call_target="tpu_custom_call" | custom-call | tf_op jit(solution)/shard_map/tensor_scatter/pallas_call | solution.py:180
  112.9 1.1 fusion.189
  115.0 12.6 %tensor_gather.9 = bf16[4,64,1024]{2,1,0:T(8,128)(2,1)} custom-call(bf16[64,1024]{1,0:T(8,128)(2,1)} %fusion.153.own_ref), custom_call_target="tpu_custom_call" | custom-call | tf_op jit(solution)/shard_map/tensor_gather/pallas_call | solution.py:99
  127.6 3.7 multiply_convert_fusion.1
  131.3 1.5 fusion.81
  132.8 14.4 %tensor_scatter.9 = f32[64,1024]{1,0:T(8,128)} custom-call(bf16[4,64,1024]{2,1,0:T(8,128)(2,1)} %bitcast.386), custom_call_target="tpu_custom_call" | custom-call | tf_op jit(solution)/shard_map/tensor_scatter/pallas_call | solution.py:180
  147.2 1.2 fusion.188
  149.4 12.7 %tensor_gather.10 = bf16[4,64,1024]{2,1,0:T(8,128)(2,1)} custom-call(bf16[64,1024]{1,0:T(8,128)(2,1)} %add_convert_fusion.1.own_ref), custom_call_target="tpu_custom_call" | custom-call | tf_op jit(solution)/shard_map/tensor_gather/pallas_call | solution.py:99
  162.1 2.4 fusion.98
  164.5 1.5 fusion.201
  166.7 1.1 convolution_convert_fusion.4
  167.8 14.8 %tensor_scatter.10 = f32[64,1024]{1,0:T(8,128)} custom-call(bf16[4,64,1024]{2,1,0:T(8,128)(2,1)} %bitcast.374), custom_call_target="tpu_custom_call" | custom-call | tf_op jit(solution)/shard_map/tensor_scatter/pallas_call | solution.py:180
  182.7 1.2 fusion.187
  184.9 13.6 %tensor_gather.11 = bf16[4,64,1024]{2,1,0:T(8,128)(2,1)} custom-call(bf16[64,1024]{1,0:T(8,128)(2,1)} %fusion.154.own_ref), custom_call_target="tpu_custom_call" | custom-call | tf_op jit(solution)/shard_map/tensor_gather/pallas_call | solution.py:99
  198.5 3.7 multiply_convert_fusion
  202.2 1.5 fusion.87
  203.7 15.5 %tensor_scatter.11 = f32[64,1024]{1,0:T(8,128)} custom-call(bf16[4,64,1024]{2,1,0:T(8,128)(2,1)} %bitcast.387), custom_call_target="tpu_custom_call" | custom-call | tf_op jit(solution)/shard_map/tensor_scatter/pallas_call | solution.py:180
  219.2 1.2 fusion.186
  225.1 12.7 %tensor_gather.12 = bf16[4,64,1024]{2,1,0:T(8,128)(2,1)} custom-call(bf16[64,1024]{1,0:T(8,128)(2,1)} %convert_element_type.280.own_ref), custom_call_target="tpu_custom_call" | custom-call | tf_op jit(solution)/shard_map/tensor_gather/pallas_call | solution.py:99
  237.8 3.8 fusion.206
  241.6 1.5 fusion.84
  243.1 14.4 %tensor_scatter.12 = f32[64,1024]{1,0:T(8,128)} custom-call(bf16[4,64,1024]{2,1,0:T(8,128)(2,1)} %bitcast.388), custom_call_target="tpu_custom_call" | custom-call | tf_op jit(solution)/shard_map/tensor_scatter/pallas_call | solution.py:180
  257.5 1.7 multiply_reduce_fusion.2
  260.6 11.9 %tensor_gather.13 = bf16[4,64,1024]{2,1,0:T(8,128)(2,1)} custom-call(bf16[64,1024]{1,0:T(8,128)(2,1)} %convert_element_type.283.own_ref), custom_call_target="tpu_custom_call" | custom-call | tf_op jit(solution)/shard_map/tensor_gather/pallas_call | solution.py:99
  272.4 1.4 convolution_convert_fusion.9
  273.9 1.4 fusion.195
  275.6 2.9 convolution_convert_fusion.8
  278.5 3.4 fusion.194
  284.1 2.9 fusion.72
  287.0 15.6 %tensor_scatter.13 = f32[64,1024]{1,0:T(8,128)} custom-call(bf16[4,64,1024]{2,1,0:T(8,128)(2,1)} %bitcast.389), custom_call_target="tpu_custom_call" | custom-call | tf_op jit(solution)/shard_map/tensor_scatter/pallas_call | solution.py:180
  302.6 1.7 multiply_reduce_fusion.3
  305.7 11.8 %tensor_gather.14 = bf16[4,64,1024]{2,1,0:T(8,128)(2,1)} custom-call(bf16[64,1024]{1,0:T(8,128)(2,1)} %convert_element_type.287.own_ref), custom_call_target="tpu_custom_call" | custom-call | tf_op jit(solution)/shard_map/tensor_gather/pallas_call | solution.py:99
  317.5 3.8 fusion.207
  321.3 1.5 fusion.78
  322.9 15.0 %tensor_scatter.14 = f32[64,1024]{1,0:T(8,128)} custom-call(bf16[4,64,1024]{2,1,0:T(8,128)(2,1)} %bitcast.384), custom_call_target="tpu_custom_call" | custom-call | tf_op jit(solution)/shard_map/tensor_scatter/pallas_call | solution.py:180
  337.9 1.7 multiply_reduce_fusion.4
  341.0 12.3 %tensor_gather.15 = bf16[4,64,1024]{2,1,0:T(8,128)(2,1)} custom-call(bf16[64,1024]{1,0:T(8,128)(2,1)} %convert_element_type.290.own_ref), custom_call_target="tpu_custom_call" | custom-call | tf_op jit(solution)/shard_map/tensor_gather/pallas_call | solution.py:99
  353.3 1.4 convolution_convert_fusion.7
  354.8 2.3 fusion.193
  357.5 2.0 convolution_convert_fusion.6
  359.4 2.6 fusion.192
  362.5 2.9 fusion.75
  365.4 15.0 %tensor_scatter.15 = f32[64,1024]{1,0:T(8,128)} custom-call(bf16[4,64,1024]{2,1,0:T(8,128)(2,1)} %bitcast.385), custom_call_target="tpu_custom_call" | custom-call | tf_op jit(solution)/shard_map/tensor_scatter/pallas_call | solution.py:180
  380.5 1.7 select_convert_fusion
  382.2 1.2 collective-permute-start.1
  383.4 1.1 fusion.105
  384.5 1.1 fusion.104
  385.6 1.8 fusion.37
  387.4 1.9 fusion.36
  390.1 2.1 convert_bitcast_fusion.2
  392.3 2.1 convert_bitcast_fusion
  394.4 2.2 convert_bitcast_fusion.3
  398.4 2.3 pad_maximum_fusion.3.refs_1_
  401.3 3.5 pad_maximum_fusion.2.refs_0_
  404.8 2.5 pad_maximum_fusion.1.refs_3_
  407.3 1.2 copy-done.2
  408.5 2.4 pad_maximum_fusion.refs_2_
  411.0 118.4 %scatter_grads.1 = (f32[3,256,256]{2,1,0:T(8,128)}, f32[256,256]{1,0:T(8,128)}, f32[256,1024]{1,0:T(8,128)}, f32[1024,256]{1,0:T(8,128)}, f32[8,128]{1,0:T(8,128...) custom-call(bf16[2,3,1024,256]{3,2,1,0:T(8,128)(2,1)} %pad_maximum_fusion.2.refs_0_, ...), custom_call_target="tpu_custom_call" | custom-call | tf_op jit(solution)/shard_map/scatter_grads/pallas_call | solution.py:501
  (318 shorter events, 42.0 us)
Async XLA Ops:
  74.5 199.3 %copy-start.50 = (pred[256,256]{0,1:T(8,128)(4,1)}, pred[256,256]{0,1:T(8,128)(4,1)S(1)}, u32[]{:S(2)}) copy-start(pred[256,256]{0,1:T(8,128)(4,1)S(1)} %broadcast_compare_fusion) | copy-start | bytes 196612
  96.0 16.9 %copy-start.81 = (f32[4,256]{1,0:T(4,128)}, f32[4,256]{1,0:T(4,128)S(1)}, u32[]{:S(2)}) copy-start(f32[4,256]{1,0:T(4,128)S(1)} %get-tuple-element.160) | copy-start | bytes 12292
  96.0 16.9 %copy-start.16 = (bf16[2,1,64,1024]{3,2,1,0:T(8,128)(2,1)S(1)}, bf16[2,1,64,1024]{3,2,1,0:T(8,128)(2,1)}, u32[]{:S(2)}) copy-start(bf16[2,1,64,1024]{3,2,1,0:T(8,128)(2,1)} %param.15) | copy-start | bytes 786436
  114.0 33.2 %copy-start.66 = (f32[64]{0:T(128)}, f32[64]{0:T(128)S(1)}, u32[]{:S(2)}) copy-start(f32[64]{0:T(128)S(1)} %broadcast_multiply_fusion.11) | copy-start | bytes 772
  114.2 33.0 %copy-start.68 = (f32[64]{0:T(128)}, f32[64]{0:T(128)S(1)}, u32[]{:S(2)}) copy-start(f32[64]{0:T(128)S(1)} %add_rsqrt_fusion.3) | copy-start | bytes 772
  131.3 18.1 %copy-start.30 = (bf16[256,1024]{1,0:T(8,128)(2,1)}, bf16[256,1024]{1,0:T(8,128)(2,1)S(1)}, u32[]{:S(2)}) copy-start(bf16[256,1024]{1,0:T(8,128)(2,1)S(1)} %get-tuple-element.162) | copy-start | bytes 1572868
  148.6 72.0 %copy-start.51 = (f32[64]{0:T(128)}, f32[64]{0:T(128)S(1)}, u32[]{:S(2)}) copy-start(f32[64]{0:T(128)S(1)} %add_rsqrt_fusion.2) | copy-start | bytes 772
  164.5 109.4 %copy-start.47 = (bf16[256,1,256]{0,2,1:T(8,128)(2,1)}, bf16[256,1,256]{0,2,1:T(8,128)(2,1)S(1)}, u32[]{:S(2)}) copy-start(bf16[256,1,256]{0,2,1:T(8,128)(2,1)S(1)} %get-tuple-element.120) | copy-start | bytes 393220
  164.5 109.4 %copy-start.49 = (bf16[256,1,256]{0,2,1:T(8,128)(2,1)}, bf16[256,1,256]{0,2,1:T(8,128)(2,1)S(1)}, u32[]{:S(2)}) copy-start(bf16[256,1,256]{0,2,1:T(8,128)(2,1)S(1)} %get-tuple-element.121) | copy-start | bytes 393220
  166.0 107.9 %copy-start.84 = (f32[4,256]{1,0:T(4,128)}, f32[4,256]{1,0:T(4,128)S(1)}, u32[]{:S(2)}) copy-start(f32[4,256]{1,0:T(4,128)S(1)} %get-tuple-element.164) | copy-start | bytes 12292
  198.5 3.7 copy-start.80
  202.2 19.4 %copy-start.32 = (bf16[256,1024]{1,0:T(8,128)(2,1)}, bf16[256,1024]{1,0:T(8,128)(2,1)S(1)}, u32[]{:S(2)}) copy-start(bf16[256,1024]{1,0:T(8,128)(2,1)S(1)} %get-tuple-element.166) | copy-start | bytes 1572868
  202.2 20.1 %copy-start.39 = (bf16[2,1,64,1024]{3,2,1,0:T(8,128)(2,1)S(1)}, bf16[2,1,64,1024]{3,2,1,0:T(8,128)(2,1)}, u32[]{:S(2)}) copy-start(bf16[2,1,64,1024]{3,2,1,0:T(8,128)(2,1)} %param.17) | copy-start | bytes 786436
  221.5 312.0 %collective-permute-start = (bf16[64,1024]{1,0:T(8,128)(2,1)}, bf16[64,1024]{1,0:T(8,128)(2,1)}, u32[]{:S(2)}, u32[]{:S(2)}) collective-permute-start(bf16[64,1024]{1,0:T(8,128)(2,1)} %get-tuple-element.106), channel_id=1, source_target_pairs={{0,16},{16,0},{1,17},{17,1},{2,18},{18,2},{3,19},{19,3},{4,20},{20... | collective-permute-start | bytes 393224 | tf_op jit(solution)/shard_map/ppermute | solution.py:774
  237.8 3.8 copy-start.77
  281.9 20.7 %copy-start.52 = (f32[64]{0:T(128)S(1)}, f32[64]{0:T(128)}, u32[]{:S(2)}) copy-start(f32[64]{0:T(128)} %copy-done.51) | copy-start | bytes 772
  283.0 3.9 copy-start.18
  317.5 3.8 copy-start.78
  321.3 16.6 %copy-start.67 = (f32[64]{0:T(128)S(1)}, f32[64]{0:T(128)}, u32[]{:S(2)}) copy-start(f32[64]{0:T(128)} %copy-done.66) | copy-start | bytes 772
  321.3 16.6 %copy-start.69 = (f32[64]{0:T(128)S(1)}, f32[64]{0:T(128)}, u32[]{:S(2)}) copy-start(f32[64]{0:T(128)} %copy-done.68) | copy-start | bytes 772
  322.8 31.9 %copy-start.42 = (bf16[256,1,256]{0,2,1:T(8,128)(2,1)S(1)}, bf16[256,1,256]{0,2,1:T(8,128)(2,1)}, u32[]{:S(2)}) copy-start(bf16[256,1,256]{0,2,1:T(8,128)(2,1)} %copy-done.41) | copy-start | bytes 393220
  322.8 31.9 %copy-start.45 = (bf16[256,1,256]{0,2,1:T(8,128)(2,1)S(1)}, bf16[256,1,256]{0,2,1:T(8,128)(2,1)}, u32[]{:S(2)}) copy-start(bf16[256,1,256]{0,2,1:T(8,128)(2,1)} %copy-done.44) | copy-start | bytes 393220
  322.9 32.0 %copy-start.82 = (f32[4,256]{1,0:T(4,128)S(1)}, f32[4,256]{1,0:T(4,128)}, u32[]{:S(2)}) copy-start(f32[4,256]{1,0:T(4,128)} %copy-done.81) | copy-start | bytes 12292
  353.3 3.8 copy-start.29
  362.1 21.3 %copy-start.7 = (bf16[4,64,1024]{2,1,0:T(8,128)(2,1)S(1)}, bf16[4,64,1024]{2,1,0:T(8,128)(2,1)}, u32[]{:S(2)}) copy-start(bf16[4,64,1024]{2,1,0:T(8,128)(2,1)} %tensor_gather.13) | copy-start | bytes 1572868
  362.5 22.0 %copy-start.8 = (bf16[4,64,1024]{2,1,0:T(8,128)(2,1)S(1)}, bf16[4,64,1024]{2,1,0:T(8,128)(2,1)}, u32[]{:S(2)}) copy-start(bf16[4,64,1024]{2,1,0:T(8,128)(2,1)} %tensor_gather.15) | copy-start | bytes 1572868
  362.5 23.1 %copy-start.6 = (bf16[4,64,1024]{2,1,0:T(8,128)(2,1)S(1)}, bf16[4,64,1024]{2,1,0:T(8,128)(2,1)}, u32[]{:S(2)}) copy-start(bf16[4,64,1024]{2,1,0:T(8,128)(2,1)} %tensor_gather.10) | copy-start | bytes 1572868
  362.5 23.1 %copy-start.19 = (bf16[256,1,256]{2,0,1:T(8,128)(2,1)S(1)}, bf16[256,1,256]{2,0,1:T(8,128)(2,1)}, u32[]{:S(2)}) copy-start(bf16[256,1,256]{2,0,1:T(8,128)(2,1)} %copy-done.18) | copy-start | bytes 393220
  362.5 23.1 %copy-start.21 = (bf16[256,1,256]{2,0,1:T(8,128)(2,1)S(1)}, bf16[256,1,256]{2,0,1:T(8,128)(2,1)}, u32[]{:S(2)}) copy-start(bf16[256,1,256]{2,0,1:T(8,128)(2,1)} %copy-done.20) | copy-start | bytes 393220
  365.4 21.9 %copy-start.5 = (bf16[4,64,1024]{2,1,0:T(8,128)(2,1)S(1)}, bf16[4,64,1024]{2,1,0:T(8,128)(2,1)}, u32[]{:S(2)}) copy-start(bf16[4,64,1024]{2,1,0:T(8,128)(2,1)} %tensor_gather.8) | copy-start | bytes 1572868
  380.4 6.9 %copy-start.23 = (bf16[256,1,256]{2,0,1:T(8,128)(2,1)S(1)}, bf16[256,1,256]{2,0,1:T(8,128)(2,1)}, u32[]{:S(2)}) copy-start(bf16[256,1,256]{2,0,1:T(8,128)(2,1)} %copy-done.22) | copy-start | bytes 393220
  380.5 6.9 %copy-start.25 = (bf16[256,1,256]{2,0,1:T(8,128)(2,1)S(1)}, bf16[256,1,256]{2,0,1:T(8,128)(2,1)}, u32[]{:S(2)}) copy-start(bf16[256,1,256]{2,0,1:T(8,128)(2,1)} %copy-done.24) | copy-start | bytes 393220
  380.5 6.9 %copy-start.27 = (bf16[256,1,256]{2,0,1:T(8,128)(2,1)S(1)}, bf16[256,1,256]{2,0,1:T(8,128)(2,1)}, u32[]{:S(2)}) copy-start(bf16[256,1,256]{2,0,1:T(8,128)(2,1)} %copy-done.26) | copy-start | bytes 393220
  382.2 153.2 %collective-permute-start.1 = (bf16[64,1024]{1,0:T(8,128)(2,1)}, bf16[64,1024]{1,0:T(8,128)(2,1)}, u32[]{:S(2)}, u32[]{:S(2)}) collective-permute-start(bf16[64,1024]{1,0:T(8,128)(2,1)} %select_convert_fusion), channel_id=1, source_target_pairs={{0,16},{16,0},{1,17},{17,1},{2,18},{18,2},{3,19},{19,3},{4,20},{20... | collective-permute-start | bytes 393224 | tf_op jit(solution)/shard_map/ppermute | solution.py:781
  384.5 4.8 copy-start.12
  384.5 4.8 copy-start.31
  390.0 4.3 copy-start.9
  390.0 4.3 copy-start.37
  392.1 4.4 copy-start.71
  392.1 4.6 copy-start.54
  392.1 4.6 copy-start.55
  392.1 4.6 copy-start.56
  392.2 4.6 copy-start.57
  392.2 4.6 copy-start.58
  392.2 4.6 copy-start.65
  392.2 4.7 copy-start.73
  392.2 4.7 copy-start.74
  392.2 4.9 copy-start.72
  392.2 5.1 copy-start.59
  392.2 5.1 copy-start.60
  392.2 5.1 copy-start.61
  392.2 5.1 copy-start.62
  392.3 5.1 copy-start.63
  392.3 5.1 copy-start.64
  392.3 5.2 copy-start.75
  392.3 5.3 copy-start.76
  404.8 3.7 copy-start.2
  411.0 122.6 %copy-start.38 = (bf16[64,1024]{1,0:T(8,128)(2,1)S(1)}, bf16[64,1024]{1,0:T(8,128)(2,1)}, u32[]{:S(2)}) copy-start(bf16[64,1024]{1,0:T(8,128)(2,1)} %get-tuple-element.107) | copy-start | bytes 393220
  411.0 122.6 %copy-start.53 = (f32[64]{0:T(128)S(1)}, f32[64]{0:T(128)}, u32[]{:S(2)}) copy-start(f32[64]{0:T(128)} %copy-done.51) | copy-start | bytes 772
  411.0 124.4 %copy-start.4 = (f32[64,1024]{1,0:T(8,128)S(1)}, f32[64,1024]{1,0:T(8,128)}, u32[]{:S(2)}) copy-start(f32[64,1024]{1,0:T(8,128)} %tensor_scatter.15) | copy-start | bytes 786436
  529.4 7.9 %copy-start.17 = (f32[3,256,256]{2,1,0:T(8,128)S(1)}, f32[3,256,256]{2,1,0:T(8,128)}, u32[]{:S(2)}) copy-start(f32[3,256,256]{2,1,0:T(8,128)} %get-tuple-element.30) | copy-start | bytes 2359300
  529.4 8.8 %copy-start.40 = (f32[256,256]{1,0:T(8,128)S(1)}, f32[256,256]{1,0:T(8,128)}, u32[]{:S(2)}) copy-start(f32[256,256]{1,0:T(8,128)} %get-tuple-element.32) | copy-start | bytes 786436
  529.4 9.5 %copy-start.15 = (f32[256,1024]{1,0:T(8,128)S(1)}, f32[256,1024]{1,0:T(8,128)}, u32[]{:S(2)}) copy-start(f32[256,1024]{1,0:T(8,128)} %get-tuple-element.34) | copy-start | bytes 3145732
  535.4 4.5 copy-start.14
  (24 other events, 62.6 us)

commit v2 on v1

--- a/solution.py
+++ b/solution.py
@@ -14,8 +14,10 @@
 VMEM_LIMIT = 60 * 1024 * 1024
 
 
-def line_barrier(me, count):
+def line_barrier(me, count, others=()):
     barrier = pltpu.get_barrier_semaphore()
+    for target in others:
+        pl.semaphore_signal(barrier, inc=1, device_id=target, device_id_type=MESH)
 
     @pl.when(me > 0)
     def _():
@@ -29,16 +31,15 @@
 
     @pl.when(inner)
     def _():
-        pl.semaphore_wait(barrier, 2)
+        pl.semaphore_wait(barrier, 2 + len(others))
 
     @pl.when(jnp.logical_not(inner))
     def _():
-        pl.semaphore_wait(barrier, 1)
-
-
-def gather_kernel(count, own_ref, all_ref, send_sem, recv_sem):
+        pl.semaphore_wait(barrier, 1 + len(others))
+
+
+def gather_steps(count, own_ref, all_ref, send_sem, recv_sem):
     me = lax.axis_index("tensor")
-    line_barrier(me, count)
 
     def copy_of(side, step):
         shard = me - step if side == 0 else me + step
@@ -84,6 +85,7 @@
 
         if step == 0:
             all_ref[me] = own_ref[...]
+        yield
     for step in range(count - 1):
         for side in range(2):
 
@@ -92,6 +94,12 @@
                 @pl.when(sends(side))
                 def _():
                     copy_of(side, step).wait_send()
+
+
+def gather_kernel(count, own_ref, all_ref, send_sem, recv_sem):
+    line_barrier(lax.axis_index("tensor"), count)
+    for _ in gather_steps(count, own_ref, all_ref, send_sem, recv_sem):
+        pass
 
 
 def tensor_gather(rows):
@@ -111,9 +119,8 @@
     return gathered.reshape(count * rows.shape[0], rows.shape[1])
 
 
-def scatter_kernel(count, part_ref, sum_ref, landed, staged, send_sem, recv_sem):
+def scatter_steps(count, part_ref, sum_ref, landed, staged, send_sem, recv_sem):
     me = lax.axis_index("tensor")
-    line_barrier(me, count)
 
     def copy_of(side, slot, first, dest):
         return pltpu.make_async_remote_copy(
@@ -139,6 +146,7 @@
             def _():
                 copy_of(side, slot, True, dest).start()
 
+    yield
     for slot in range(count - 1):
         for side in range(2):
             dest, passes, first = roles(side, slot)
@@ -151,6 +159,7 @@
                 ).astype(BF16)
                 copy_of(side, slot, False, dest).start()
 
+        yield
     for place in range(count):
 
         @pl.when(me == place)
@@ -171,6 +180,12 @@
             @pl.when(passes)
             def _():
                 copy_of(side, slot, False, dest).wait_send()
+
+
+def scatter_kernel(count, part_ref, sum_ref, landed, staged, send_sem, recv_sem):
+    line_barrier(lax.axis_index("tensor"), count)
+    for _ in scatter_steps(count, part_ref, sum_ref, landed, staged, send_sem, recv_sem):
+        pass
 
 
 def tensor_scatter(parts):
@@ -232,7 +247,8 @@
     section, dp = place
     if form == "rows":
         rows = shape[-2]
-        at = pl.ds(pl.multiple_of(dp * rows, rows), rows)
+        low, high = half or (0, rows)
+        at = pl.ds(pl.multiple_of(dp * rows + low, high - low), high - low)
         return (section, slice(None), at) if len(shape) == 3 else (section, at)
     if form == "columns":
         low, high = half
@@ -246,12 +262,7 @@
     return (section, dp)
 
 
-def weights_kernel(pieces, count, dp_count, *refs):
-    own = refs[:count]
-    full = refs[count : 2 * count]
-    send_sem, recv_sem, local_sem = refs[2 * count :]
-    cube = Cube(dp_count)
-    cube.greet()
+def weights_steps(pieces, cube, own, full, send_sem, recv_sem, local_sem):
 
     def source(piece):
         which, form, shape, half, kind = piece
@@ -291,9 +302,8 @@
         copy = pltpu.make_async_copy(source(piece), slot(piece, 0), local_sem.at[number])
         copy.start()
         locals_.append(copy)
-    rounds = cube.size
-    waited = [set() for _ in pieces]
-    for turn in range(rounds):
+    yield
+    for turn in range(cube.size - 1):
         for number, piece in enumerate(pieces):
             relays = [(m, b) for m, b in steps(piece)]
             landing = [m for m, b in relays]
@@ -305,6 +315,7 @@
             for later, bit in relays:
                 if later ^ (1 << bit) == mask and later != 1 << bit:
                     copy_of(number, piece, later, bit).start()
+        yield
     for number, piece in enumerate(pieces):
         for mask, bit in steps(piece):
             copy_of(number, piece, mask, bit).wait_send()
@@ -334,29 +345,77 @@
     return pieces
 
 
-def gather_weights(arrays, forms):
+def halves_of(forms, shapes):
+    pieces = []
+    for which, (form, shape) in enumerate(zip(forms, shapes)):
+        if len(shape) == 2 and shape[0] >= 64:
+            middle = shape[0] // 2
+            first = 1 if len(shapes) > 1 else 0
+            pieces.append((which, form, shape, (0, middle), first))
+            pieces.append((which, form, shape, (middle, shape[0]), 1))
+        else:
+            pieces.append((which, form, shape, None, 0))
+    return pieces
+
+
+def joint_kernel(scatters, line, pieces, count, dp_count, *refs):
+    cube = Cube(dp_count)
+    line_barrier(
+        lax.axis_index("tensor"), line, [cube.device(1 << bit) for bit in range(cube.bits)]
+    )
+    rows, own = refs[0], refs[1 : 1 + count]
+    result, full = refs[1 + count], refs[2 + count : 2 + 2 * count]
+    rest = refs[2 + 2 * count :]
+    steps = scatter_steps if scatters else gather_steps
+    tensor = steps(line, rows, result, *rest[3:])
+    weights = weights_steps(pieces, cube, own, full, *rest[:3])
+    running = [tensor, weights]
+    while running:
+        for one in list(running):
+            if next(one, "end") == "end":
+                running.remove(one)
+
+
+def joint_link(number, rows, arrays, forms):
+    line = lax.axis_size("tensor")
     dp_count = lax.axis_size("dp")
+    scatters = number % 2 == 1
     shapes = [array.shape for array in arrays]
-    pieces = pieces_of(forms, shapes)
+    pieces = halves_of(forms, shapes)
     count = len(arrays)
-    return pl.pallas_call(
-        functools.partial(weights_kernel, pieces, count, dp_count),
-        out_shape=[
+    depth, width = rows.shape
+    line_sems = [pltpu.SemaphoreType.DMA((2, line - 1)), pltpu.SemaphoreType.DMA((2, line - 1))]
+    if scatters:
+        depth = depth // line
+        rows = rows.reshape(line, depth, width)
+        result = jax.ShapeDtypeStruct((depth, width), F32)
+        line_scratch = [pltpu.VMEM((2, line - 1, depth, width), BF16)] * 2 + line_sems
+    else:
+        result = jax.ShapeDtypeStruct((line, depth, width), rows.dtype)
+        line_scratch = line_sems
+    results = pl.pallas_call(
+        functools.partial(joint_kernel, scatters, line, pieces, count, dp_count),
+        out_shape=[result]
+        + [
             jax.ShapeDtypeStruct(full_shape(form, shape, dp_count), BF16)
             for form, shape in zip(forms, shapes)
         ],
-        in_specs=[VMEM_SPEC] * count,
-        out_specs=[VMEM_SPEC] * count,
+        in_specs=[VMEM_SPEC] * (1 + count),
+        out_specs=[VMEM_SPEC] * (1 + count),
         scratch_shapes=[
             pltpu.SemaphoreType.DMA((len(pieces), 2 * dp_count)),
             pltpu.SemaphoreType.DMA((len(pieces), 2 * dp_count)),
             pltpu.SemaphoreType.DMA((len(pieces),)),
-        ],
+        ]
+        + line_scratch,
         compiler_params=pltpu.CompilerParams(
-            collective_id=3, has_side_effects=True, vmem_limit_bytes=VMEM_LIMIT
+            collective_id=5 + number, has_side_effects=True, vmem_limit_bytes=VMEM_LIMIT
         ),
-        name="gather_weights",
-    )(*arrays)
+        name="joint_link",
+    )(rows, *arrays)
+    if scatters:
+        return results[0], results[1:]
+    return results[0].reshape(line * depth, width), results[1:]
 
 
 def piece_shape(piece):
@@ -560,9 +619,9 @@
     return qkv_held[:, which].reshape(qkv_held.shape[0], head_count, head_size)
 
 
-def layer_forward(local_rows, pack_ids, weights):
-    qkv_mat, qv_shift, out_mat, up_mat, up_shift, down_mat, row_params = weights
-    gathered = tensor_gather(local_rows)
+def layer_forward(local_rows, pack_ids, link, weights):
+    gathered = link(0, local_rows)
+    qkv_mat, qv_shift, out_mat, up_shift, row_params = weights(0)
     tokens = gathered.shape[0]
     width = qkv_mat.shape[2]
     head_count = qv_shift.shape[1]
@@ -589,18 +648,20 @@
         .astype(jnp.bfloat16)
     )
     params_wide = row_params.astype(jnp.float32)
-    attn_part = tensor_scatter(jnp.dot(context, out_mat, preferred_element_type=jnp.float32).astype(jnp.bfloat16))
+    attn_part = link(1, jnp.dot(context, out_mat, preferred_element_type=jnp.float32).astype(jnp.bfloat16))
     resid_one = local_rows.astype(jnp.float32) + attn_part + params_wide[0]
     normed_one, scaled_one = normalize(resid_one)
     hidden_one = normed_one * params_wide[1] + params_wide[2]
-    hidden_in = tensor_gather(hidden_one.astype(jnp.bfloat16))
+    up_mat = weights(1)
+    hidden_in = link(2, hidden_one.astype(jnp.bfloat16))
+    down_mat = weights(2)
     pre_act = jnp.dot(hidden_in, up_mat, preferred_element_type=jnp.float32) + up_shift.astype(
         jnp.float32
     ).reshape(-1)
     activated = gelu_exact(pre_act).astype(jnp.bfloat16)
     resid_two = (
         hidden_one
-        + tensor_scatter(jnp.dot(activated, down_mat, preferred_element_type=jnp.float32).astype(jnp.bfloat16))
+        + link(3, jnp.dot(activated, down_mat, preferred_element_type=jnp.float32).astype(jnp.bfloat16))
         + params_wide[3]
     )
     normed_two, scaled_two = normalize(resid_two)
@@ -742,18 +803,32 @@
             jnp.zeros((small_rows * 128 - sum(small_sizes),), BF16),
         ]
     ).reshape(small_rows, 128)
-    stacked = gather_weights(
-        (jnp.swapaxes(qkv_weight[0], 0, 1), out_weight[0], up_weight[0], down_weight[0], small),
-        forms,
-    )
-
-    def layer_weights(which):
-        qkv_full, out_full, up_full, down_full, small_full = [array[which] for array in stacked]
-        if columns == "stack":
-            out_full, down_full = [
-                jnp.moveaxis(array, 0, 1).reshape(array.shape[1], -1)
-                for array in (out_full, down_full)
-            ]
+    carried = {
+        0: ((jnp.swapaxes(qkv_weight[0], 0, 1), out_weight[0], small), ["rows", columns, "stack"]),
+        1: ((up_weight[0],), ["rows"]),
+        2: ((down_weight[0],), [columns]),
+    }
+    stacked = {}
+
+    def link_first(number, array):
+        if number not in carried:
+            return tensor_scatter(array)
+        result, stacked[number] = joint_link(number, array, *carried[number])
+        return result
+
+    def link_plain(number, array):
+        return tensor_scatter(array) if number % 2 else tensor_gather(array)
+
+    def joined(array):
+        return array if columns != "stack" else jnp.moveaxis(array, 0, 1).reshape(array.shape[1], -1)
+
+    def layer_weights(which, number):
+        if number == 1:
+            return stacked[1][0][which]
+        if number == 2:
+            return joined(stacked[2][0][which])
+        qkv_full, out_full, small_full = [array[which] for array in stacked[0]]
+        out_full = joined(out_full)
         flat = small_full.reshape(dp_count, -1)
         qv_full = flat[:, : small_sizes[0]].reshape(dp_count, 2, heads, head_part)
         qv_full = jnp.moveaxis(qv_full, 0, 2).reshape(2, heads, dp_count * head_part)
@@ -762,22 +837,28 @@
         up_shift = jnp.moveaxis(up_shift, 0, 1).reshape(groups, dp_count * unit_part)
         row_params = flat[:, middle : middle + small_sizes[2]].reshape(dp_count, 6, part)
         row_params = jnp.moveaxis(row_params, 0, 1).reshape(6, dp_count * part)
-        return (qkv_full, qv_full, out_full, up_full, up_shift, down_full, row_params)
-
-    weights = [layer_weights(0), layer_weights(1)]
+        return (qkv_full, qv_full, out_full, up_shift, row_params)
+
+    def all_weights(which):
+        qkv_mat, qv_shift, out_mat, up_shift, row_params = layer_weights(which, 0)
+        up_mat, down_mat = layer_weights(which, 1), layer_weights(which, 2)
+        return (qkv_mat, qv_shift, out_mat, up_mat, up_shift, down_mat, row_params)
+
     rows = jnp.where(first, block_input[0, 0], block_input[1, 0])
     ids = jnp.where(first, seq_ids[0, 0], seq_ids[1, 0])
     upstream = jnp.where(first, out_cotangent[0, 0], out_cotangent[1, 0]).astype(F32)
-    out_first, saved_first = layer_forward(rows, ids, weights[0])
-    out_last, saved_last = layer_forward(out_first, ids, weights[1])
+    out_first, saved_first = layer_forward(rows, ids, link_first, functools.partial(layer_weights, 0))
+    out_last, saved_last = layer_forward(
+        out_first, ids, link_plain, functools.partial(layer_weights, 1)
+    )
     swap = [(0, 1), (1, 0)]
     other_out = lax.ppermute(jnp.where(first, out_last, out_first), "section", swap)
     own_out = jnp.where(first, out_first, out_last)
     section_outputs = jnp.stack(
         [jnp.where(first, own_out, other_out), jnp.where(first, other_out, own_out)]
     )
-    grad_last, mats_last, rows_last = layer_backward(upstream, ids, weights[1], saved_last)
-    grad_first, mats_first, rows_first = layer_backward(grad_last, ids, weights[0], saved_first)
+    grad_last, mats_last, rows_last = layer_backward(upstream, ids, all_weights(1), saved_last)
+    grad_first, mats_first, rows_first = layer_backward(grad_last, ids, all_weights(0), saved_first)
     other_grad = lax.ppermute(
         jnp.where(first, grad_last, grad_first).astype(BF16), "section", swap
     ).astype(F32)

time: 542 us -> 510 us (0.941)
  Pallas kernels: 404 us -> 372 us
    pallas_call x8 -> x6, Pallas kernels: 102 us -> 76.6 us  [tensor_gather(): pl.pallas_call(functools.partial(gather_kernel, count), out_shape=jax.Sha...]
    pallas_call x1 -> x3, Pallas kernels: 64 us -> 83.4 us  [joint_link(): pl.pallas_call(functools.partial(joint_kernel, scatters, line, pieces, co...]
    pallas_call x8 -> x7, Pallas kernels: 120 us -> 106 us  [tensor_scatter(): pl.pallas_call(functools.partial(scatter_kernel, count), out_shape=jax.Sh...]
    pallas_call x1, Pallas kernels: 118 us -> 106 us  [scatter_grads(): pl.pallas_call(functools.partial(grads_kernel, pieces, count, dp_count, l...]
  transfers between devices with their start and end apart: 2 -> 2, of which waited for: 0 -> 0; matrix products, arithmetic and copies ran while one was open for 15% -> 16% of each run, Pallas kernels for 42% -> 42%
where the time goes in v2:
time: 510 us; the launch traced here: 508 us
  Pallas kernels  372 us (73%)
  matrix products  68.7 us (13%)
  other arithmetic  44.9 us (9%)
  local copies, waits for them, and re-layouts  18.5 us (4%)
    pallas_call x1, Pallas kernels, scatter_grads(): pl.pallas_call(functools.partial(grads_kernel, pieces, count, dp_count, l...  106 us
    pallas_call x7, Pallas kernels, tensor_scatter(): pl.pallas_call(functools.partial(scatter_kernel, count), out_shape=jax.Sh...  106 us
    pallas_call x3, Pallas kernels, joint_link(): pl.pallas_call(functools.partial(joint_kernel, scatters, line, pieces, co...  83.4 us
    pallas_call x6, Pallas kernels, tensor_gather(): pl.pallas_call(functools.partial(gather_kernel, count), out_shape=jax.Sha...  76.6 us
    another operation x6, other arithmetic, shards(): jnp.stack(pair)  11.9 us
  transfers between devices with their start and end apart: 2, of which 0 were waited for; matrix products, arithmetic and copies ran while one was open for 16% of the time, Pallas kernels for 42%

profile of v2, /device:TPU:1, one launch (start us, length us, event | category | flops | bytes accessed | tf_op | source)
XLA Modules:
  0.0 508.4 jit_solution(721067900062646443)
XLA Ops:
  6.4 1.6 select_bitcast_fusion.2.refs_0_
  10.4 30.2 %joint_link.3 = (bf16[4,64,1024]{2,1,0:T(8,128)(2,1)}, bf16[2,3,1024,256]{3,2,1,0:T(8,128)(2,1)}, bf16[2,256,1024]{2,1,0:T(8,128)(2,1)}, bf16[2,4,16,128]{3,2,1,0:T(8,128)(2,1)}) custom-call(bf16[64,1024]{1,0:T(8,128)(2,1)} %select_bitcast_fusion.2.refs_0_, bf16[3,256,256]{2,1,0:T(8,128)(2,1)} %bitcast.394, bf16[256,256]{1,0:T(8,128)(2,1)} %bitcast.402, ...), custom_call_target="tpu_custom_call" | custom-call | tf_op jit(solution)/shard_map/joint_link/pallas_call | solution.py:396
  43.4 2.4 fusion.101
  45.9 1.5 fusion.200
  48.1 1.1 convolution_convert_fusion.5
  49.3 26.6 %joint_link.4 = (f32[64,1024]{1,0:T(8,128)}, bf16[2,1024,1024]{2,1,0:T(8,128)(2,1)}) custom-call(bf16[4,64,1024]{2,1,0:T(8,128)(2,1)} %bitcast.369, bf16[256,1024]{1,0:T(8,128)(2,1)} %bitcast.387), custom_call_target="tpu_custom_call" | custom-call | tf_op jit(solution)/shard_map/joint_link/pallas_call | solution.py:396
  75.9 1.1 fusion.189
  78.0 26.7 %joint_link.5 = (bf16[4,64,1024]{2,1,0:T(8,128)(2,1)}, bf16[2,1024,1024]{2,1,0:T(8,128)(2,1)}) custom-call(bf16[64,1024]{1,0:T(8,128)(2,1)} %fusion.153.refs_0_, bf16[1024,256]{1,0:T(8,128)(2,1)} %bitcast.380), custom_call_target="tpu_custom_call" | custom-call | tf_op jit(solution)/shard_map/joint_link/pallas_call | solution.py:396
  104.7 3.7 multiply_convert_fusion.1
  108.3 1.5 fusion.81
  109.9 17.0 %tensor_scatter.7 = f32[64,1024]{1,0:T(8,128)} custom-call(bf16[4,64,1024]{2,1,0:T(8,128)(2,1)} %bitcast.383), custom_call_target="tpu_custom_call" | custom-call | tf_op jit(solution)/shard_map/tensor_scatter/pallas_call | solution.py:195
  126.9 1.2 fusion.188
  129.1 13.2 %tensor_gather.6 = bf16[4,64,1024]{2,1,0:T(8,128)(2,1)} custom-call(bf16[64,1024]{1,0:T(8,128)(2,1)} %add_convert_fusion.1.own_ref), custom_call_target="tpu_custom_call" | custom-call | tf_op jit(solution)/shard_map/tensor_gather/pallas_call | solution.py:107
  142.3 2.4 fusion.98
  144.7 1.5 fusion.201
  146.9 1.1 convolution_convert_fusion.4
  148.1 14.8 %tensor_scatter.8 = f32[64,1024]{1,0:T(8,128)} custom-call(bf16[4,64,1024]{2,1,0:T(8,128)(2,1)} %bitcast.370), custom_call_target="tpu_custom_call" | custom-call | tf_op jit(solution)/shard_map/tensor_scatter/pallas_call | solution.py:195
  162.9 1.2 fusion.187
  165.1 14.7 %tensor_gather.7 = bf16[4,64,1024]{2,1,0:T(8,128)(2,1)} custom-call(bf16[64,1024]{1,0:T(8,128)(2,1)} %fusion.154.own_ref), custom_call_target="tpu_custom_call" | custom-call | tf_op jit(solution)/shard_map/tensor_gather/pallas_call | solution.py:107
  179.9 3.8 multiply_convert_fusion
  183.6 1.5 fusion.87
  185.2 14.4 %tensor_scatter.9 = f32[64,1024]{1,0:T(8,128)} custom-call(bf16[4,64,1024]{2,1,0:T(8,128)(2,1)} %bitcast.384), custom_call_target="tpu_custom_call" | custom-call | tf_op jit(solution)/shard_map/tensor_scatter/pallas_call | solution.py:195
  199.5 1.2 fusion.186
  205.3 12.1 %tensor_gather.8 = bf16[4,64,1024]{2,1,0:T(8,128)(2,1)} custom-call(bf16[64,1024]{1,0:T(8,128)(2,1)} %convert_element_type.280.own_ref), custom_call_target="tpu_custom_call" | custom-call | tf_op jit(solution)/shard_map/tensor_gather/pallas_call | solution.py:107
  217.5 3.7 fusion.206
  221.2 1.5 fusion.84
  222.8 15.9 %tensor_scatter.10 = f32[64,1024]{1,0:T(8,128)} custom-call(bf16[4,64,1024]{2,1,0:T(8,128)(2,1)} %bitcast.385), custom_call_target="tpu_custom_call" | custom-call | tf_op jit(solution)/shard_map/tensor_scatter/pallas_call | solution.py:195
  238.7 1.7 multiply_reduce_fusion.2
  241.8 12.8 %tensor_gather.9 = bf16[4,64,1024]{2,1,0:T(8,128)(2,1)} custom-call(bf16[64,1024]{1,0:T(8,128)(2,1)} %convert_element_type.283.own_ref), custom_call_target="tpu_custom_call" | custom-call | tf_op jit(solution)/shard_map/tensor_gather/pallas_call | solution.py:107
  254.6 1.4 convolution_convert_fusion.9
  256.1 1.4 fusion.195
  257.9 2.7 convolution_convert_fusion.8
  260.5 3.2 fusion.194
  265.9 2.9 fusion.72
  268.8 14.7 %tensor_scatter.11 = f32[64,1024]{1,0:T(8,128)} custom-call(bf16[4,64,1024]{2,1,0:T(8,128)(2,1)} %bitcast.386), custom_call_target="tpu_custom_call" | custom-call | tf_op jit(solution)/shard_map/tensor_scatter/pallas_call | solution.py:195
  283.5 1.7 multiply_reduce_fusion.3
  286.5 11.9 %tensor_gather.10 = bf16[4,64,1024]{2,1,0:T(8,128)(2,1)} custom-call(bf16[64,1024]{1,0:T(8,128)(2,1)} %convert_element_type.287.own_ref), custom_call_target="tpu_custom_call" | custom-call | tf_op jit(solution)/shard_map/tensor_gather/pallas_call | solution.py:107
  298.4 3.8 fusion.207
  302.2 1.5 fusion.78
  303.7 14.4 %tensor_scatter.12 = f32[64,1024]{1,0:T(8,128)} custom-call(bf16[4,64,1024]{2,1,0:T(8,128)(2,1)} %bitcast.381), custom_call_target="tpu_custom_call" | custom-call | tf_op jit(solution)/shard_map/tensor_scatter/pallas_call | solution.py:195
  318.2 1.7 multiply_reduce_fusion.4
  321.3 11.8 %tensor_gather.11 = bf16[4,64,1024]{2,1,0:T(8,128)(2,1)} custom-call(bf16[64,1024]{1,0:T(8,128)(2,1)} %convert_element_type.290.own_ref), custom_call_target="tpu_custom_call" | custom-call | tf_op jit(solution)/shard_map/tensor_gather/pallas_call | solution.py:107
  333.1 1.4 convolution_convert_fusion.7
  334.6 2.3 fusion.193
  337.3 2.0 convolution_convert_fusion.6
  339.2 2.6 fusion.192
  342.3 2.9 fusion.75
  345.2 14.6 %tensor_scatter.13 = f32[64,1024]{1,0:T(8,128)} custom-call(bf16[4,64,1024]{2,1,0:T(8,128)(2,1)} %bitcast.382), custom_call_target="tpu_custom_call" | custom-call | tf_op jit(solution)/shard_map/tensor_scatter/pallas_call | solution.py:195
  359.8 1.7 select_convert_fusion
  361.5 1.5 collective-permute-start.1
  363.0 1.1 fusion.105
  364.1 1.1 fusion.104
  365.2 1.8 fusion.37
  367.0 1.8 fusion.36
  369.6 2.1 convert_bitcast_fusion.2
  371.9 2.1 convert_bitcast_fusion
  374.0 2.1 convert_bitcast_fusion.3
  377.9 2.3 pad_maximum_fusion.3.refs_1_
  380.8 3.6 pad_maximum_fusion.2.refs_0_
  384.4 2.5 pad_maximum_fusion.1.refs_3_
  386.9 1.2 copy-done.2
  388.2 2.3 pad_maximum_fusion.refs_2_
  390.5 106.4 %scatter_grads.1 = (f32[3,256,256]{2,1,0:T(8,128)}, f32[256,256]{1,0:T(8,128)}, f32[256,1024]{1,0:T(8,128)}, f32[1024,256]{1,0:T(8,128)}, f32[8,128]{1,0:T(8,128...) custom-call(bf16[2,3,1024,256]{3,2,1,0:T(8,128)(2,1)} %pad_maximum_fusion.2.refs_0_, ...), custom_call_target="tpu_custom_call" | custom-call | tf_op jit(solution)/shard_map/scatter_grads/pallas_call | solution.py:560
  501.2 1.1 select_bitcast_fusion.1
  (317 shorter events, 40.9 us)
Async XLA Ops:
  42.3 213.8 %copy-start.50 = (pred[256,256]{0,1:T(8,128)(4,1)}, pred[256,256]{0,1:T(8,128)(4,1)S(1)}, u32[]{:S(2)}) copy-start(pred[256,256]{0,1:T(8,128)(4,1)S(1)} %broadcast_compare_fusion) | copy-start | bytes 196612
  47.4 28.5 %copy-start.81 = (f32[4,256]{1,0:T(4,128)}, f32[4,256]{1,0:T(4,128)S(1)}, u32[]{:S(2)}) copy-start(f32[4,256]{1,0:T(4,128)S(1)} %get-tuple-element.166) | copy-start | bytes 12292
  47.4 28.5 %copy-start.14 = (bf16[2,1,64,1024]{3,2,1,0:T(8,128)(2,1)S(1)}, bf16[2,1,64,1024]{3,2,1,0:T(8,128)(2,1)}, u32[]{:S(2)}) copy-start(bf16[2,1,64,1024]{3,2,1,0:T(8,128)(2,1)} %param.15) | copy-start | bytes 786436
  77.0 49.9 %copy-start.66 = (f32[64]{0:T(128)}, f32[64]{0:T(128)S(1)}, u32[]{:S(2)}) copy-start(f32[64]{0:T(128)S(1)} %broadcast_multiply_fusion.11) | copy-start | bytes 772
  77.2 49.7 %copy-start.68 = (f32[64]{0:T(128)}, f32[64]{0:T(128)S(1)}, u32[]{:S(2)}) copy-start(f32[64]{0:T(128)S(1)} %add_rsqrt_fusion.3) | copy-start | bytes 772
  108.3 20.8 %copy-start.30 = (bf16[256,1024]{1,0:T(8,128)(2,1)}, bf16[256,1024]{1,0:T(8,128)(2,1)S(1)}, u32[]{:S(2)}) copy-start(bf16[256,1024]{1,0:T(8,128)(2,1)S(1)} %get-tuple-element.168) | copy-start | bytes 1572868
  128.3 72.6 %copy-start.51 = (f32[64]{0:T(128)}, f32[64]{0:T(128)S(1)}, u32[]{:S(2)}) copy-start(f32[64]{0:T(128)S(1)} %add_rsqrt_fusion.2) | copy-start | bytes 772
  144.7 111.3 %copy-start.47 = (bf16[256,1,256]{0,2,1:T(8,128)(2,1)}, bf16[256,1,256]{0,2,1:T(8,128)(2,1)S(1)}, u32[]{:S(2)}) copy-start(bf16[256,1,256]{0,2,1:T(8,128)(2,1)S(1)} %get-tuple-element.126) | copy-start | bytes 393220
  144.7 111.3 %copy-start.49 = (bf16[256,1,256]{0,2,1:T(8,128)(2,1)}, bf16[256,1,256]{0,2,1:T(8,128)(2,1)S(1)}, u32[]{:S(2)}) copy-start(bf16[256,1,256]{0,2,1:T(8,128)(2,1)S(1)} %get-tuple-element.127) | copy-start | bytes 393220
  146.2 109.9 %copy-start.84 = (f32[4,256]{1,0:T(4,128)}, f32[4,256]{1,0:T(4,128)S(1)}, u32[]{:S(2)}) copy-start(f32[4,256]{1,0:T(4,128)S(1)} %get-tuple-element.170) | copy-start | bytes 12292
  179.9 3.8 copy-start.80
  183.6 18.2 %copy-start.32 = (bf16[256,1024]{1,0:T(8,128)(2,1)}, bf16[256,1024]{1,0:T(8,128)(2,1)S(1)}, u32[]{:S(2)}) copy-start(bf16[256,1024]{1,0:T(8,128)(2,1)S(1)} %get-tuple-element.172) | copy-start | bytes 1572868
  183.6 18.9 %copy-start.39 = (bf16[2,1,64,1024]{3,2,1,0:T(8,128)(2,1)S(1)}, bf16[2,1,64,1024]{3,2,1,0:T(8,128)(2,1)}, u32[]{:S(2)}) copy-start(bf16[2,1,64,1024]{3,2,1,0:T(8,128)(2,1)} %param.17) | copy-start | bytes 786436
  201.8 299.3 %collective-permute-start = (bf16[64,1024]{1,0:T(8,128)(2,1)}, bf16[64,1024]{1,0:T(8,128)(2,1)}, u32[]{:S(2)}, u32[]{:S(2)}) collective-permute-start(bf16[64,1024]{1,0:T(8,128)(2,1)} %get-tuple-element.112), channel_id=1, source_target_pairs={{0,16},{16,0},{1,17},{17,1},{2,18},{18,2},{3,19},{19,3},{4,20},{20... | collective-permute-start | bytes 393224 | tf_op jit(solution)/shard_map/ppermute | solution.py:855
  217.5 3.8 copy-start.77
  263.7 19.7 %copy-start.52 = (f32[64]{0:T(128)S(1)}, f32[64]{0:T(128)}, u32[]{:S(2)}) copy-start(f32[64]{0:T(128)} %copy-done.51) | copy-start | bytes 772
  264.8 3.9 copy-start.17
  298.4 3.8 copy-start.78
  302.2 16.0 %copy-start.67 = (f32[64]{0:T(128)S(1)}, f32[64]{0:T(128)}, u32[]{:S(2)}) copy-start(f32[64]{0:T(128)} %copy-done.66) | copy-start | bytes 772
  302.2 16.0 %copy-start.69 = (f32[64]{0:T(128)S(1)}, f32[64]{0:T(128)}, u32[]{:S(2)}) copy-start(f32[64]{0:T(128)} %copy-done.68) | copy-start | bytes 772
  303.7 30.9 %copy-start.42 = (bf16[256,1,256]{0,2,1:T(8,128)(2,1)S(1)}, bf16[256,1,256]{0,2,1:T(8,128)(2,1)}, u32[]{:S(2)}) copy-start(bf16[256,1,256]{0,2,1:T(8,128)(2,1)} %copy-done.41) | copy-start | bytes 393220
  303.7 30.9 %copy-start.45 = (bf16[256,1,256]{0,2,1:T(8,128)(2,1)S(1)}, bf16[256,1,256]{0,2,1:T(8,128)(2,1)}, u32[]{:S(2)}) copy-start(bf16[256,1,256]{0,2,1:T(8,128)(2,1)} %copy-done.44) | copy-start | bytes 393220
  303.7 30.9 %copy-start.82 = (f32[4,256]{1,0:T(4,128)S(1)}, f32[4,256]{1,0:T(4,128)}, u32[]{:S(2)}) copy-start(f32[4,256]{1,0:T(4,128)} %copy-done.81) | copy-start | bytes 12292
  333.1 3.8 copy-start.28
  341.9 21.1 %copy-start.6 = (bf16[4,64,1024]{2,1,0:T(8,128)(2,1)S(1)}, bf16[4,64,1024]{2,1,0:T(8,128)(2,1)}, u32[]{:S(2)}) copy-start(bf16[4,64,1024]{2,1,0:T(8,128)(2,1)} %tensor_gather.9) | copy-start | bytes 1572868
  342.2 21.8 %copy-start.7 = (bf16[4,64,1024]{2,1,0:T(8,128)(2,1)S(1)}, bf16[4,64,1024]{2,1,0:T(8,128)(2,1)}, u32[]{:S(2)}) copy-start(bf16[4,64,1024]{2,1,0:T(8,128)(2,1)} %tensor_gather.11) | copy-start | bytes 1572868
  342.2 22.9 %copy-start.5 = (bf16[4,64,1024]{2,1,0:T(8,128)(2,1)S(1)}, bf16[4,64,1024]{2,1,0:T(8,128)(2,1)}, u32[]{:S(2)}) copy-start(bf16[4,64,1024]{2,1,0:T(8,128)(2,1)} %tensor_gather.6) | copy-start | bytes 1572868
  342.3 22.9 %copy-start.18 = (bf16[256,1,256]{2,0,1:T(8,128)(2,1)S(1)}, bf16[256,1,256]{2,0,1:T(8,128)(2,1)}, u32[]{:S(2)}) copy-start(bf16[256,1,256]{2,0,1:T(8,128)(2,1)} %copy-done.17) | copy-start | bytes 393220
  342.3 22.9 %copy-start.20 = (bf16[256,1,256]{2,0,1:T(8,128)(2,1)S(1)}, bf16[256,1,256]{2,0,1:T(8,128)(2,1)}, u32[]{:S(2)}) copy-start(bf16[256,1,256]{2,0,1:T(8,128)(2,1)} %copy-done.19) | copy-start | bytes 393220
  345.2 21.8 %copy-start.16 = (bf16[4,64,1024]{2,1,0:T(8,128)(2,1)S(1)}, bf16[4,64,1024]{2,1,0:T(8,128)(2,1)}, u32[]{:S(2)}) copy-start(bf16[4,64,1024]{2,1,0:T(8,128)(2,1)} %get-tuple-element.28) | copy-start | bytes 1572868
  359.8 7.2 %copy-start.22 = (bf16[256,1,256]{2,0,1:T(8,128)(2,1)S(1)}, bf16[256,1,256]{2,0,1:T(8,128)(2,1)}, u32[]{:S(2)}) copy-start(bf16[256,1,256]{2,0,1:T(8,128)(2,1)} %copy-done.21) | copy-start | bytes 393220
  359.8 7.2 %copy-start.24 = (bf16[256,1,256]{2,0,1:T(8,128)(2,1)S(1)}, bf16[256,1,256]{2,0,1:T(8,128)(2,1)}, u32[]{:S(2)}) copy-start(bf16[256,1,256]{2,0,1:T(8,128)(2,1)} %copy-done.23) | copy-start | bytes 393220
  359.8 7.1 %copy-start.26 = (bf16[256,1,256]{2,0,1:T(8,128)(2,1)S(1)}, bf16[256,1,256]{2,0,1:T(8,128)(2,1)}, u32[]{:S(2)}) copy-start(bf16[256,1,256]{2,0,1:T(8,128)(2,1)} %copy-done.25) | copy-start | bytes 393220
  361.5 141.5 %collective-permute-start.1 = (bf16[64,1024]{1,0:T(8,128)(2,1)}, bf16[64,1024]{1,0:T(8,128)(2,1)}, u32[]{:S(2)}, u32[]{:S(2)}) collective-permute-start(bf16[64,1024]{1,0:T(8,128)(2,1)} %select_convert_fusion), channel_id=1, source_target_pairs={{0,16},{16,0},{1,17},{17,1},{2,18},{18,2},{3,19},{19,3},{4,20},{20... | collective-permute-start | bytes 393224 | tf_op jit(solution)/shard_map/ppermute | solution.py:862
  364.1 4.7 copy-start.10
  364.1 4.7 copy-start.31
  369.6 4.4 copy-start.29
  369.6 4.4 copy-start.37
  371.7 4.4 copy-start.71
  371.7 4.5 copy-start.54
  371.7 4.5 copy-start.55
  371.7 4.5 copy-start.56
  371.7 4.5 copy-start.57
  371.7 4.5 copy-start.58
  371.7 4.5 copy-start.65
  371.7 4.6 copy-start.73
  371.8 4.7 copy-start.74
  371.8 4.9 copy-start.72
  371.8 5.1 copy-start.59
  371.8 5.1 copy-start.60
  371.8 5.1 copy-start.61
  371.8 5.1 copy-start.62
  371.8 5.1 copy-start.63
  371.8 5.1 copy-start.64
  371.8 5.2 %copy-start.75 = (f32[4,64]{1,0:T(4,128)S(1)}, f32[4,64]{1,0:T(4,128)}, u32[]{:S(2)}) copy-start(f32[4,64]{1,0:T(4,128)} %get-tuple-element.134) | copy-start | bytes 3076
  371.8 5.2 %copy-start.76 = (f32[4,64]{1,0:T(4,128)S(1)}, f32[4,64]{1,0:T(4,128)}, u32[]{:S(2)}) copy-start(f32[4,64]{1,0:T(4,128)} %get-tuple-element.132) | copy-start | bytes 3076
  384.4 3.7 copy-start.2
  390.5 110.7 %copy-start.38 = (bf16[64,1024]{1,0:T(8,128)(2,1)S(1)}, bf16[64,1024]{1,0:T(8,128)(2,1)}, u32[]{:S(2)}) copy-start(bf16[64,1024]{1,0:T(8,128)(2,1)} %get-tuple-element.113) | copy-start | bytes 393220
  390.5 110.7 %copy-start.53 = (f32[64]{0:T(128)S(1)}, f32[64]{0:T(128)}, u32[]{:S(2)}) copy-start(f32[64]{0:T(128)} %copy-done.51) | copy-start | bytes 772
  390.5 112.5 %copy-start.4 = (f32[64,1024]{1,0:T(8,128)S(1)}, f32[64,1024]{1,0:T(8,128)}, u32[]{:S(2)}) copy-start(f32[64,1024]{1,0:T(8,128)} %tensor_scatter.13) | copy-start | bytes 786436
  496.9 7.9 %copy-start.15 = (f32[3,256,256]{2,1,0:T(8,128)S(1)}, f32[3,256,256]{2,1,0:T(8,128)}, u32[]{:S(2)}) copy-start(f32[3,256,256]{2,1,0:T(8,128)} %get-tuple-element.36) | copy-start | bytes 2359300
  497.0 8.8 %copy-start.40 = (f32[256,256]{1,0:T(8,128)S(1)}, f32[256,256]{1,0:T(8,128)}, u32[]{:S(2)}) copy-start(f32[256,256]{1,0:T(8,128)} %get-tuple-element.38) | copy-start | bytes 786436
  497.0 9.5 %copy-start.13 = (f32[256,1024]{1,0:T(8,128)S(1)}, f32[256,1024]{1,0:T(8,128)}, u32[]{:S(2)}) copy-start(f32[256,1024]{1,0:T(8,128)} %get-tuple-element.40) | copy-start | bytes 3145732
  503.0 4.5 copy-start.12
  (24 other events, 62.2 us)
